TPU v7x, 32 devices: a whole 2x2x4 slice. The times are simulated.
32 devices in a mesh: seq: 4 (over z), batch: 8 (over y, x, core).
Axes of the slice: x: 2, y: 2, z: 4, core: 2. Of those that a mesh axis runs over, the one named last changes fastest.
Arguments:
- queries: bfloat16 [8, 1024, 1024], P('batch', 'seq'), may hold values from -80 to 80
- keys: bfloat16 [8, 1024, 1024], P('batch', 'seq'), may hold values from -8 to 8
- values: bfloat16 [8, 1024, 1024], P('batch', 'seq'), may hold values from -6 to 6
- residual: bfloat16 [8, 1024, 1024], P('batch', 'seq'), may hold values from -2 to 2
- out_weight: bfloat16 [1024, 1024], replicated, may hold values from -0.1875 to 0.1875
- norm_gain: float32 [1024], replicated, may hold values from 0.1 to 1.9
- source_queue: bfloat16 [4096, 1024], P('batch'), may hold values from -32 to 32
- span_lengths: int32 [8, 64], P('batch'), may hold values from 1 to 32, 1024 in all within a row
- positives: int32 [8, 64], P(None, 'seq'), may hold values from 0 to 4095
Outputs:
- anchors: bfloat16 [8, 64, 1024], P('batch', 'seq')
- losses: float32 [8, 64], P('batch', 'seq')
All inputs are finite; a program needn't handle non-finite values.
Results may differ from a plain program's by a relative error of at most 0.0047.
Values may be sent and summed in bfloat16 or wider, within the bound.
A program may use at most 64 MiB of HBM per device.

v0:
```python
import math

import jax
import jax.numpy as jnp
from jax import lax
from jax.sharding import PartitionSpec as P

HEADS = 16
WINDOW = 512


logit_scale = 20.0


def shifted(array, axis, by):
    devices = lax.axis_size(axis)
    pairs = [(i, i + by) for i in range(devices) if 0 <= i + by < devices]
    return lax.ppermute(array, axis, pairs)


def body(
    queries, keys, values, residual, out_weight, norm_gain, source_queue, span_lengths, positives
):
    tok_rows = queries.shape[1]
    model_width = queries.shape[2]
    head_count = HEADS
    head_size = model_width // head_count
    reach_back = (WINDOW - 1) // tok_rows + 1
    seq_index = lax.axis_index("seq")
    seq_count = lax.axis_size("seq")
    first_pos = seq_index * tok_rows
    own_pair = jnp.stack([keys[0], values[0]])
    earlier = []
    for hop_count in range(1, reach_back + 1):
        earlier.append(shifted(own_pair, "seq", hop_count))
    ordered = earlier[::-1] + [own_pair]
    keys_all = jnp.concatenate([item[0] for item in ordered], axis=0)
    values_all = jnp.concatenate([item[1] for item in ordered], axis=0)
    query_pos = first_pos + jnp.arange(tok_rows, dtype=jnp.int32)
    key_pos = (
        first_pos - reach_back * tok_rows + jnp.arange((reach_back + 1) * tok_rows, dtype=jnp.int32)
    )
    distance = query_pos[:, None] - key_pos[None, :]
    allowed = (distance >= 0) & (distance < WINDOW) & (key_pos[None, :] >= 0)
    group_size = 4
    group_cols = group_size * head_size
    key_rows = keys_all.shape[0]

    def attend_group(group_index):
        first_col = group_index * group_cols
        query_group = lax.dynamic_slice_in_dim(queries[0], first_col, group_cols, 1).reshape(
            tok_rows, group_size, head_size
        )
        key_group = lax.dynamic_slice_in_dim(keys_all, first_col, group_cols, 1).reshape(
            key_rows, group_size, head_size
        )
        value_group = lax.dynamic_slice_in_dim(values_all, first_col, group_cols, 1).reshape(
            key_rows, group_size, head_size
        )
        scores = jnp.einsum(
            "qhd,khd->hqk", query_group, key_group, preferred_element_type=jnp.float32
        ) / math.sqrt(head_size)
        scores = jnp.where(allowed[None], scores, -jnp.inf)
        row_peak = jnp.max(scores, axis=-1, keepdims=True)
        exp_scores = jnp.exp(scores - row_peak)
        weights = (exp_scores / jnp.sum(exp_scores, axis=-1, keepdims=True)).astype(jnp.bfloat16)
        mixed = jnp.einsum("hqk,khd->qhd", weights, value_group, preferred_element_type=jnp.float32)
        return mixed.astype(jnp.bfloat16).reshape(tok_rows, group_cols)

    blocks = lax.map(attend_group, jnp.arange(head_count // group_size, dtype=jnp.int32))
    attended = jnp.transpose(blocks, (1, 0, 2)).reshape(tok_rows, model_width)
    hidden = residual[0].astype(jnp.float32) + jnp.dot(
        attended, out_weight, preferred_element_type=jnp.float32
    )
    scale = lax.rsqrt(jnp.mean(hidden * hidden, axis=-1, keepdims=True) + 1e-05)
    normed = (hidden * scale * norm_gain).astype(jnp.bfloat16)
    lengths = span_lengths[0]
    span_ends = jnp.cumsum(lengths)
    starts = span_ends - lengths
    own_rows = positives.shape[1]
    row_ids = jnp.arange(own_rows * lax.axis_size("seq"), dtype=jnp.int32)
    listed = row_ids % own_rows * seq_count + row_ids // own_rows
    begin_at = jnp.take(starts, listed)
    end_at = jnp.take(span_ends, listed)
    member = (
        (query_pos[None, :] >= begin_at[:, None]) & (query_pos[None, :] < end_at[:, None])
    ).astype(jnp.bfloat16)
    pooled = lax.psum_scatter(
        jnp.dot(member, normed, preferred_element_type=jnp.float32),
        "seq",
        scatter_dimension=0,
        tiled=True,
    )
    anchors = (pooled * lax.rsqrt(jnp.sum(pooled * pooled, axis=-1, keepdims=True) + 1e-06)).astype(
        jnp.bfloat16
    )
    batch_index = lax.axis_index("batch")
    queue_rows = source_queue.shape[0]
    queue_ids = batch_index * queue_rows + jnp.arange(queue_rows, dtype=jnp.int32)
    wanted_all = positives.reshape(-1)
    logits = logit_scale * lax.dot_general(
        lax.all_gather(anchors, "batch", axis=0, tiled=True),
        source_queue,
        (((1,), (1,)), ((), ())),
        preferred_element_type=jnp.float32,
    )
    row_peak = jnp.max(logits, axis=1)
    row_total = jnp.sum(jnp.exp(logits - row_peak[:, None]), axis=1)
    positive = jnp.sum(jnp.where(wanted_all[:, None] == queue_ids[None, :], logits, 0.0), axis=1)
    score_stats = jnp.stack([row_peak, row_total, positive])
    row_peak = score_stats[0]
    row_total = score_stats[1]
    positive = score_stats[2]
    by_owner = (
        lax.all_to_all(
            row_peak.reshape(-1, own_rows), "batch", split_axis=0, concat_axis=0, tiled=True
        ),
        lax.all_to_all(
            row_total.reshape(-1, own_rows), "batch", split_axis=0, concat_axis=0, tiled=True
        ),
        lax.all_to_all(
            positive.reshape(-1, own_rows), "batch", split_axis=0, concat_axis=0, tiled=True
        ),
    )
    global_peak = jnp.max(by_owner[0], axis=0)
    own_total = jnp.sum(by_owner[1] * jnp.exp(by_owner[0] - global_peak[None, :]), axis=0)
    own_positive = jnp.sum(by_owner[2], axis=0)
    losses = global_peak + jnp.log(own_total) - own_positive
    return (anchors[None], losses[None])


def solution(mesh):
    return jax.shard_map(
        body,
        mesh=mesh,
        in_specs=(
            P("batch", "seq", None),
            P("batch", "seq", None),
            P("batch", "seq", None),
            P("batch", "seq", None),
            P(),
            P(),
            P("batch", None),
            P("batch", None),
            P(None, "seq"),
        ),
        out_specs=(P("batch", "seq", None), P("batch", "seq")),
        check_vma=False,
    )
```

profile of v0, /device:TPU:0, one launch (start us, length us, event | category | flops | bytes accessed | tf_op | source)
XLA Modules:
  0.0 194.9 jit_solution(13899965426699623206)
XLA Ops:
  11.0 7.0 %collective-permute-start = (bf16[2,256,1024]{1,2,0:T(8,128)(2,1)}, bf16[2,256,1024]{1,2,0:T(8,128)(2,1)}, u32[]{:S(2)}, u32[]{:S(2)}) collective-permute-start(bf16[2,256,1024]{1,2,0:T(8,128)(2,1)} %pad_maximum_fusion.2), channel_id=1, source_target_pairs={{0,16},{8,24},{1,17},{9,25},{2,18},{10,26},{3,19},{11,27},{4,20},{... | collective-permute-start | bytes 3145736 | tf_op jit(solution)/shard_map/ppermute | solution.py:18
  17.9 4.5 %collective-permute-start.1 = (bf16[2,256,1024]{1,2,0:T(8,128)(2,1)}, bf16[2,256,1024]{1,2,0:T(8,128)(2,1)}, u32[]{:S(2)}, u32[]{:S(2)}) collective-permute-start(bf16[2,256,1024]{1,2,0:T(8,128)(2,1)} %pad_maximum_fusion.2), channel_id=1, source_target_pairs={{0,8},{8,16},{16,24},{1,9},{9,17},{17,25},{2,10},{10,18},{18,26},{... | collective-permute-start | bytes 3145736 | tf_op jit(solution)/shard_map/ppermute | solution.py:18
  24.4 16.5 %collective-permute-done = bf16[2,256,1024]{1,2,0:T(8,128)(2,1)} collective-permute-done((bf16[2,256,1024]{1,2,0:T(8,128)(2,1)}, bf16[2,256,1024]{1,2,0:T(8,128)(2,1)}, u32[]{:S(2)}, u32[]{:S(2)}) %collective-permute-start) | collective-permute-done | bytes 1048608 | tf_op jit(solution)/shard_map/ppermute | solution.py:18
  42.1 20.1 %collective-permute-done.1 = bf16[2,256,1024]{1,2,0:T(8,128)(2,1)} collective-permute-done((bf16[2,256,1024]{1,2,0:T(8,128)(2,1)}, bf16[2,256,1024]{1,2,0:T(8,128)(2,1)}, u32[]{:S(2)}, u32[]{:S(2)}) %collective-permute-start.1) | collective-permute-done | bytes 1048608 | tf_op jit(solution)/shard_map/ppermute | solution.py:18
  63.4 1.8 pad_maximum_fusion
  65.3 39.3 %while.11 = (s32[]{:T(128)}, bf16[4,256,256]{1,2,0:T(8,128)(2,1)}, s32[4]{0:T(128)S(1)}, bf16[768,1024]{0,1:T(8,128)(2,1)}, bf16[1,256,1024]{2,1,0:T(8,128)(2,1)...) while((s32[]{:T(128)}, bf16[4,256,256]{1,2,0:T(8,128)(2,1)}, ...), condition=%wide.region_4.6_spmd.clone, body=%wide.region_1.5_spmd.clone.sunk | while | flops 207094528 | bytes 10106303 | solution.py:70
  69.0 2.9 %fusion.48 = (f32[4,256]{1,0:T(4,128)S(1)}, f32[4,256,768]{2,1,0:T(8,128)}) fusion(pred[256,768]{1,0:T(8,128)(4,1)S(1)} %fusion.47, bf16[256,4,64]{0,2,1:T(8,128)(2,1)S(1)} %bitcast.64, bf16[768,4,64]{0,2,1:T(8,128)(2,1)S(1)} %bitcast.61), kind=kOutput, calls=%fused_computation.69.clone.1 | convolution fusion | flops 103809792 | bytes 3870720 | tf_op jit(solution)/shard_map/while/body/eval_jaxpr/sub | solution.py:65
  71.9 2.6 %fusion.49 = bf16[4,64,256]{2,1,0:T(8,128)(2,1)S(1)} fusion(bf16[768,4,64]{0,2,1:T(8,128)(2,1)S(1)} %bitcast.60, f32[4,256,768]{2,1,0:T(8,128)} %get-tuple-element.188, f32[4,256]{1,0:T(4,128)S(1)} %get-tuple-element.189), kind=kOutput, calls=%fused_computation.12.clone.1 | convolution fusion | flops 102301696 | bytes 3674112 | tf_op jit(solution)/shard_map/while/body/eval_jaxpr/hqk,khd->qhd/dot_general | solution.py:67
  78.8 2.9 %fusion.48 = (f32[4,256]{1,0:T(4,128)S(1)}, f32[4,256,768]{2,1,0:T(8,128)}) fusion(pred[256,768]{1,0:T(8,128)(4,1)S(1)} %fusion.47, bf16[256,4,64]{0,2,1:T(8,128)(2,1)S(1)} %bitcast.64, bf16[768,4,64]{0,2,1:T(8,128)(2,1)S(1)} %bitcast.61), kind=kOutput, calls=%fused_computation.69.clone.1 | convolution fusion | flops 103809792 | bytes 3870720 | tf_op jit(solution)/shard_map/while/body/eval_jaxpr/sub | solution.py:65
  81.7 2.6 %fusion.49 = bf16[4,64,256]{2,1,0:T(8,128)(2,1)S(1)} fusion(bf16[768,4,64]{0,2,1:T(8,128)(2,1)S(1)} %bitcast.60, f32[4,256,768]{2,1,0:T(8,128)} %get-tuple-element.188, f32[4,256]{1,0:T(4,128)S(1)} %get-tuple-element.189), kind=kOutput, calls=%fused_computation.12.clone.1 | convolution fusion | flops 102301696 | bytes 3674112 | tf_op jit(solution)/shard_map/while/body/eval_jaxpr/hqk,khd->qhd/dot_general | solution.py:67
  88.6 2.9 %fusion.48 = (f32[4,256]{1,0:T(4,128)S(1)}, f32[4,256,768]{2,1,0:T(8,128)}) fusion(pred[256,768]{1,0:T(8,128)(4,1)S(1)} %fusion.47, bf16[256,4,64]{0,2,1:T(8,128)(2,1)S(1)} %bitcast.64, bf16[768,4,64]{0,2,1:T(8,128)(2,1)S(1)} %bitcast.61), kind=kOutput, calls=%fused_computation.69.clone.1 | convolution fusion | flops 103809792 | bytes 3870720 | tf_op jit(solution)/shard_map/while/body/eval_jaxpr/sub | solution.py:65
  91.5 2.6 %fusion.49 = bf16[4,64,256]{2,1,0:T(8,128)(2,1)S(1)} fusion(bf16[768,4,64]{0,2,1:T(8,128)(2,1)S(1)} %bitcast.60, f32[4,256,768]{2,1,0:T(8,128)} %get-tuple-element.188, f32[4,256]{1,0:T(4,128)S(1)} %get-tuple-element.189), kind=kOutput, calls=%fused_computation.12.clone.1 | convolution fusion | flops 102301696 | bytes 3674112 | tf_op jit(solution)/shard_map/while/body/eval_jaxpr/hqk,khd->qhd/dot_general | solution.py:67
  98.5 2.9 %fusion.48 = (f32[4,256]{1,0:T(4,128)S(1)}, f32[4,256,768]{2,1,0:T(8,128)}) fusion(pred[256,768]{1,0:T(8,128)(4,1)S(1)} %fusion.47, bf16[256,4,64]{0,2,1:T(8,128)(2,1)S(1)} %bitcast.64, bf16[768,4,64]{0,2,1:T(8,128)(2,1)S(1)} %bitcast.61), kind=kOutput, calls=%fused_computation.69.clone.1 | convolution fusion | flops 103809792 | bytes 3870720 | tf_op jit(solution)/shard_map/while/body/eval_jaxpr/sub | solution.py:65
  101.3 2.6 %fusion.49 = bf16[4,64,256]{2,1,0:T(8,128)(2,1)S(1)} fusion(bf16[768,4,64]{0,2,1:T(8,128)(2,1)S(1)} %bitcast.60, f32[4,256,768]{2,1,0:T(8,128)} %get-tuple-element.188, f32[4,256]{1,0:T(4,128)S(1)} %get-tuple-element.189), kind=kOutput, calls=%fused_computation.12.clone.1 | convolution fusion | flops 102301696 | bytes 3674112 | tf_op jit(solution)/shard_map/while/body/eval_jaxpr/hqk,khd->qhd/dot_general | solution.py:67
  104.6 2.1 %multiply_reduce_fusion = (f32[256]{0:T(256)S(1)}, f32[256,1024]{1,0:T(8,128)S(1)}) fusion(bf16[256,1024]{0,1:T(8,128)(2,1)} %bitcast.66, bf16[1024,1024]{1,0:T(8,128)(2,1)S(1)} %copy-done, bf16[1,256,1024]{2,1,0:T(8,128)(2,1)} %param.16), kind=kOutput, calls=%fused_computation.30 | convolution fusion | flops 537919232 | bytes 4195328 | tf_op jit(solution)/shard_map/dot_general | solution.py:72
  107.8 43.5 %reduce-scatter.2.cloned.1.call-done = f32[16,1024]{1,0:T(8,128)} async-done(((f32[64,1024]{1,0:T(8,128)}), f32[16,1024]{1,0:T(8,128)}) %reduce-scatter.2.cloned.1.call-update) | async-done | bytes 65552 | tf_op jit(solution)/shard_map/reduce_scatter | solution.py:88
  153.3 9.3 %all_gather.3 = bf16[128,1024]{1,0:T(8,128)(2,1)S(1)} all-gather(bf16[16,1024]{1,0:T(8,128)(2,1)S(1)} %multiply_convert_fusion.2), channel_id=1, replica_groups=mesh['seq'=4,'batch'=8] {'batch'}, dimensions={0}, use_global_device_ids=true | all-gather | bytes 294912 | tf_op jit(solution)/shard_map/all_gather | solution.py:102
  163.8 3.3 %all-to-all-start = ((f32[8,1,16]{2,1,0:T(1,128)}), f32[8,1,16]{2,1,0:T(1,128)S(1)}, u32[]{:S(2)}, u32[]{:S(2)}) async-start(f32[8,1,16]{2,1,0:T(1,128)} %bitcast.12), calls=%async_computation.1 | async-start | bytes 8192 | tf_op jit(solution)/shard_map/all_to_all | solution.py:115
  168.0 3.6 %all-to-all-done = f32[8,1,16]{2,1,0:T(1,128)S(1)} async-done(((f32[8,1,16]{2,1,0:T(1,128)}), f32[8,1,16]{2,1,0:T(1,128)S(1)}, u32[]{:S(2)}, u32[]{:S(2)}) %all-to-all-start) | async-done | bytes 544 | tf_op jit(solution)/shard_map/all_to_all | solution.py:115
  171.6 3.3 %all-to-all-start.1 = ((f32[8,1,16]{2,1,0:T(1,128)}), f32[8,1,16]{2,1,0:T(1,128)S(1)}, u32[]{:S(2)}, u32[]{:S(2)}) async-start(f32[8,1,16]{2,1,0:T(1,128)} %bitcast.13), calls=%async_computation.2 | async-start | bytes 8192 | tf_op jit(solution)/shard_map/all_to_all | solution.py:118
  175.0 1.5 fusion.37
  177.2 2.4 %all-to-all-done.1 = f32[8,1,16]{2,1,0:T(1,128)S(1)} async-done(((f32[8,1,16]{2,1,0:T(1,128)}), f32[8,1,16]{2,1,0:T(1,128)S(1)}, u32[]{:S(2)}, u32[]{:S(2)}) %all-to-all-start.1) | async-done | bytes 544 | tf_op jit(solution)/shard_map/all_to_all | solution.py:118
  179.6 3.2 %all-to-all-start.2 = ((f32[8,1,16]{2,1,0:T(1,128)}), f32[8,1,16]{2,1,0:T(1,128)S(1)}, u32[]{:S(2)}, u32[]{:S(2)}) async-start(f32[8,1,16]{2,1,0:T(1,128)} %bitcast.16), calls=%async_computation.3 | async-start | bytes 8192 | tf_op jit(solution)/shard_map/all_to_all | solution.py:121
  182.9 4.6 %all-to-all-done.2 = f32[8,1,16]{2,1,0:T(1,128)S(1)} async-done(((f32[8,1,16]{2,1,0:T(1,128)}), f32[8,1,16]{2,1,0:T(1,128)S(1)}, u32[]{:S(2)}, u32[]{:S(2)}) %all-to-all-start.2) | async-done | bytes 544 | tf_op jit(solution)/shard_map/all_to_all | solution.py:121
  (71 shorter events, 29.4 us)
Async XLA Ops:
  7.2 97.4 %copy-start = (bf16[1024,1024]{1,0:T(8,128)(2,1)S(1)}, bf16[1024,1024]{1,0:T(8,128)(2,1)}, u32[]{:S(2)}) copy-start(bf16[1024,1024]{1,0:T(8,128)(2,1)} %param.17) | copy-start | bytes 6291460
  7.2 15.2 %copy-start.4 = (s32[1,64]{1,0:T(1,128)S(1)}, s32[1,64]{1,0:T(1,128)}, u32[]{:S(2)}) copy-start(s32[1,64]{1,0:T(1,128)} %param.20) | copy-start | bytes 772
  7.2 144.2 %reduce-scatter.2.cloned.1.call-start = ((), (), s32[]{:S(2)}) async-start(), calls=%async_computation.4 | async-start | bytes 327680 | tf_op jit(solution)/shard_map/reduce_scatter | solution.py:88
  11.0 29.9 %collective-permute-start = (bf16[2,256,1024]{1,2,0:T(8,128)(2,1)}, bf16[2,256,1024]{1,2,0:T(8,128)(2,1)}, u32[]{:S(2)}, u32[]{:S(2)}) collective-permute-start(bf16[2,256,1024]{1,2,0:T(8,128)(2,1)} %pad_maximum_fusion.2), channel_id=1, source_target_pairs={{0,16},{8,24},{1,17},{9,25},{2,18},{10,26},{3,19},{11,27},{4,20},{... | collective-permute-start | bytes 3145736 | tf_op jit(solution)/shard_map/ppermute | solution.py:18
  17.9 44.2 %collective-permute-start.1 = (bf16[2,256,1024]{1,2,0:T(8,128)(2,1)}, bf16[2,256,1024]{1,2,0:T(8,128)(2,1)}, u32[]{:S(2)}, u32[]{:S(2)}) collective-permute-start(bf16[2,256,1024]{1,2,0:T(8,128)(2,1)} %pad_maximum_fusion.2), channel_id=1, source_target_pairs={{0,8},{8,16},{16,24},{1,9},{9,17},{17,25},{2,10},{10,18},{18,26},{... | collective-permute-start | bytes 3145736 | tf_op jit(solution)/shard_map/ppermute | solution.py:18
  104.6 2.1 %copy-start.2 = (f32[1024]{0:T(1024)S(1)}, f32[1024]{0:T(1024)}, u32[]{:S(2)}) copy-start(f32[1024]{0:T(1024)} %param.18) | copy-start | bytes 12292
  104.6 3.2 %copy-start.3 = (s32[8,16]{1,0:T(8,128)S(1)}, s32[8,16]{1,0:T(8,128)}, u32[]{:S(2)}) copy-start(s32[8,16]{1,0:T(8,128)} %param.21) | copy-start | bytes 1540
  104.6 58.0 %copy-start.1 = (bf16[512,1024]{1,0:T(8,128)(2,1)S(1)}, bf16[512,1024]{1,0:T(8,128)(2,1)}, u32[]{:S(2)}) copy-start(bf16[512,1024]{1,0:T(8,128)(2,1)} %param.19) | copy-start | bytes 3145732
  163.8 7.9 %all-to-all-start = ((f32[8,1,16]{2,1,0:T(1,128)}), f32[8,1,16]{2,1,0:T(1,128)S(1)}, u32[]{:S(2)}, u32[]{:S(2)}) async-start(f32[8,1,16]{2,1,0:T(1,128)} %bitcast.12), calls=%async_computation.1 | async-start | bytes 8192 | tf_op jit(solution)/shard_map/all_to_all | solution.py:115
  171.6 8.0 %all-to-all-start.1 = ((f32[8,1,16]{2,1,0:T(1,128)}), f32[8,1,16]{2,1,0:T(1,128)S(1)}, u32[]{:S(2)}, u32[]{:S(2)}) async-start(f32[8,1,16]{2,1,0:T(1,128)} %bitcast.13), calls=%async_computation.2 | async-start | bytes 8192 | tf_op jit(solution)/shard_map/all_to_all | solution.py:118
  179.6 7.9 %all-to-all-start.2 = ((f32[8,1,16]{2,1,0:T(1,128)}), f32[8,1,16]{2,1,0:T(1,128)S(1)}, u32[]{:S(2)}, u32[]{:S(2)}) async-start(f32[8,1,16]{2,1,0:T(1,128)} %bitcast.16), calls=%async_computation.3 | async-start | bytes 8192 | tf_op jit(solution)/shard_map/all_to_all | solution.py:121
Sparse Core Ops, SparseCore 0:
  107.9 43.4 reduce-scatter.1
where the time goes:
time: 196 us; the launch traced here: 195 us
  waiting for transfers between devices  90.7 us (46%)
  matrix products  25.4 us (13%)
  local copies, waits for them, and re-layouts  22.7 us (12%)
  starting transfers between devices  21.4 us (11%)
  between operations  14.2 us (7%)
  blocking collectives  9.26 us (5%)
  other arithmetic  8.48 us (4%)
  loops' own time  2.72 us (1%)
    reduce_scatter x1, waiting for transfers between devices, body(): lax.psum_scatter(jnp.dot(member, normed, preferred_element_type=jnp.float...  43.5 us
    ppermute x2, waiting for transfers between devices, shifted(): return lax.ppermute(array, axis, pairs)  36.5 us
    sub x4, matrix products, attend_group(): exp_scores = jnp.exp(scores - row_peak)  11.5 us
    ppermute x2, starting transfers between devices, shifted(): return lax.ppermute(array, axis, pairs)  11.5 us
    dot_general x4, matrix products, attend_group(): jnp.einsum('hqk,khd->qhd', weights, value_group, preferred_element_type=j...  10.3 us
    all_gather x1, blocking collectives, body(): lax.all_gather(anchors, 'batch', axis=0, tiled=True)  9.26 us
    dynamic_slice x4, local copies, waits for them, and re-layouts, attend_group(): lax.dynamic_slice_in_dim(keys_all, first_col, group_cols, 1)  4.68 us
    all_to_all x1, waiting for transfers between devices, body(): lax.all_to_all(positive.reshape(-1, own_rows), 'batch', split_axis=0, con...  4.6 us
  transfers between devices with their start and end apart: 6, of which 6 were waited for; matrix products, arithmetic and copies ran while one was open for 3% of the time, Pallas kernels for 0%

commit v1 on v0

v1 whole, which is shorter than its diff:
```python
import functools
import math

import jax
import jax.numpy as jnp
from jax import lax
from jax.experimental import pallas as pl
from jax.experimental.pallas import tpu as pltpu
from jax.sharding import PartitionSpec as P

HEADS = 16
WINDOW = 512
MESH = pl.DeviceIdType.MESH
F32 = jnp.float32
BF16 = jnp.bfloat16


logit_scale = 20.0


def shifted(array, axis, by):
    devices = lax.axis_size(axis)
    pairs = [(i, i + by) for i in range(devices) if 0 <= i + by < devices]
    return lax.ppermute(array, axis, pairs)


def tail_kernel(
    n_seq,
    n_batch,
    attended_ref,
    residual_ref,
    gain_ref,
    lengths_ref,
    wanted_ref,
    weight_hbm,
    queue_hbm,
    anchors_ref,
    losses_ref,
    weight,
    queue,
    parts,
    parts_in,
    anchors_all,
    stats,
    load_sem,
    part_send,
    part_recv,
    anchor_send,
    anchor_recv,
    stat_send,
    stat_recv,
):
    seq = lax.axis_index("seq")
    batch = lax.axis_index("batch")
    weight_load = pltpu.make_async_copy(weight_hbm, weight, load_sem.at[0])
    queue_load = pltpu.make_async_copy(queue_hbm, queue, load_sem.at[1])
    weight_load.start()
    queue_load.start()
    seq_peers = [lax.rem(seq + d, n_seq) for d in range(1, n_seq)]
    batch_peers = [lax.rem(batch + d, n_batch) for d in range(1, n_batch)]
    barrier = pltpu.get_barrier_semaphore()
    for peer in seq_peers:
        pl.semaphore_signal(barrier, inc=1, device_id={"seq": peer}, device_id_type=MESH)
    for peer in batch_peers:
        pl.semaphore_signal(barrier, inc=1, device_id={"batch": peer}, device_id_type=MESH)

    tok_rows = attended_ref.shape[0]
    own_rows, width = anchors_ref.shape
    funcs = own_rows * n_seq
    weight_load.wait()
    hidden = residual_ref[...].astype(F32) + jnp.dot(
        attended_ref[...], weight[...], preferred_element_type=F32
    )
    scale = lax.rsqrt(jnp.mean(hidden * hidden, axis=-1, keepdims=True) + 1e-05)
    normed = (hidden * scale * gain_ref[...]).astype(BF16)

    row_ids = lax.broadcasted_iota(jnp.int32, (funcs, funcs), 0)
    func_ids = lax.broadcasted_iota(jnp.int32, (funcs, funcs), 1)
    listed = lax.rem(row_ids, own_rows) * n_seq + row_ids // own_rows
    lengths = jnp.broadcast_to(lengths_ref[...].astype(F32), (funcs, funcs))
    begin_at = jnp.sum(jnp.where(func_ids < listed, lengths, 0.0), axis=1, keepdims=True)
    end_at = jnp.sum(jnp.where(func_ids <= listed, lengths, 0.0), axis=1, keepdims=True)
    pos = (
        seq * tok_rows + lax.broadcasted_iota(jnp.int32, (funcs, tok_rows), 1)
    ).astype(F32)
    member = jnp.where((pos >= begin_at) & (pos < end_at), 1.0, 0.0).astype(BF16)
    partial = jnp.dot(member, normed, preferred_element_type=F32)
    parts[...] = partial.reshape(n_seq, own_rows, width).astype(BF16)

    pl.semaphore_wait(barrier, n_seq - 1 + n_batch - 1)
    copies = []
    for d in range(1, n_seq):
        copy = pltpu.make_async_remote_copy(
            src_ref=parts.at[seq_peers[d - 1]],
            dst_ref=parts_in.at[d - 1],
            send_sem=part_send.at[d - 1],
            recv_sem=part_recv.at[d - 1],
            device_id={"seq": seq_peers[d - 1]},
            device_id_type=MESH,
        )
        copy.start()
        copies.append(copy)
    pooled = parts[seq].astype(F32)
    for d in range(1, n_seq):
        copies[d - 1].wait_recv()
        pooled = pooled + parts_in[d - 1].astype(F32)
    anchors = (
        pooled * lax.rsqrt(jnp.sum(pooled * pooled, axis=-1, keepdims=True) + 1e-06)
    ).astype(BF16)
    anchors_ref[...] = anchors
    anchors_all[batch] = anchors
    for copy in copies:
        copy.wait_send()

    copies = []
    for d in range(1, n_batch):
        copy = pltpu.make_async_remote_copy(
            src_ref=anchors_all.at[batch],
            dst_ref=anchors_all.at[batch],
            send_sem=anchor_send.at[d - 1],
            recv_sem=anchor_recv.at[d - 1],
            device_id={"batch": batch_peers[d - 1]},
            device_id_type=MESH,
        )
        copy.start()
        copies.append(copy)
    queue_load.wait()
    for copy in copies:
        copy.wait()
    rows = n_batch * own_rows
    logits = logit_scale * lax.dot_general(
        queue[...],
        anchors_all[...].reshape(rows, width),
        (((1,), (1,)), ((), ())),
        preferred_element_type=F32,
    )
    queue_rows = queue.shape[0]
    queue_ids = batch * queue_rows + lax.broadcasted_iota(jnp.int32, logits.shape, 0)
    row_peak = jnp.max(logits, axis=0, keepdims=True)
    row_total = jnp.sum(jnp.exp(logits - row_peak), axis=0, keepdims=True)
    positive = jnp.sum(
        jnp.where(wanted_ref[...] == queue_ids, logits, 0.0), axis=0, keepdims=True
    )
    stats[batch] = jnp.concatenate(
        [row_peak, row_total, positive, jnp.zeros((5, rows), F32)], axis=0
    )
    copies = []
    for d in range(1, n_batch):
        copy = pltpu.make_async_remote_copy(
            src_ref=stats.at[batch],
            dst_ref=stats.at[batch],
            send_sem=stat_send.at[d - 1],
            recv_sem=stat_recv.at[d - 1],
            device_id={"batch": batch_peers[d - 1]},
            device_id_type=MESH,
        )
        copy.start()
        copies.append(copy)
    for copy in copies:
        copy.wait()
    peaks = [stats[b, 0:1, :] for b in range(n_batch)]
    top = functools.reduce(jnp.maximum, peaks)
    total = sum(stats[b, 1:2, :] * jnp.exp(peaks[b] - top) for b in range(n_batch))
    chosen = sum(stats[b, 2:3, :] for b in range(n_batch))
    loss = top + jnp.log(total) - chosen
    loss_col = jnp.sum(
        jnp.where(
            lax.broadcasted_iota(jnp.int32, (own_rows, rows), 1)
            == batch * own_rows + lax.broadcasted_iota(jnp.int32, (own_rows, rows), 0),
            jnp.broadcast_to(loss, (own_rows, rows)),
            0.0,
        ),
        axis=1,
        keepdims=True,
    )
    losses_ref[...] = jnp.broadcast_to(loss_col, losses_ref.shape)


def tail(n_seq, n_batch, attended, residual, gain, lengths, wanted, weight, queue, own_rows):
    width = attended.shape[1]
    rows = n_batch * own_rows
    vmem = pl.BlockSpec(memory_space=pltpu.VMEM)
    hbm = pl.BlockSpec(memory_space=pl.ANY)
    return pl.pallas_call(
        functools.partial(tail_kernel, n_seq, n_batch),
        out_shape=(
            jax.ShapeDtypeStruct((own_rows, width), BF16),
            jax.ShapeDtypeStruct((own_rows, 128), F32),
        ),
        in_specs=[vmem] * 5 + [hbm] * 2,
        out_specs=(vmem, vmem),
        scratch_shapes=[
            pltpu.VMEM(weight.shape, BF16),
            pltpu.VMEM(queue.shape, BF16),
            pltpu.VMEM((n_seq, own_rows, width), BF16),
            pltpu.VMEM((n_seq - 1, own_rows, width), BF16),
            pltpu.VMEM((n_batch, own_rows, width), BF16),
            pltpu.VMEM((n_batch, 8, rows), F32),
            pltpu.SemaphoreType.DMA((2,)),
            pltpu.SemaphoreType.DMA((n_seq - 1,)),
            pltpu.SemaphoreType.DMA((n_seq - 1,)),
            pltpu.SemaphoreType.DMA((n_batch - 1,)),
            pltpu.SemaphoreType.DMA((n_batch - 1,)),
            pltpu.SemaphoreType.DMA((n_batch - 1,)),
            pltpu.SemaphoreType.DMA((n_batch - 1,)),
        ],
        compiler_params=pltpu.CompilerParams(
            collective_id=0, has_side_effects=True, vmem_limit_bytes=40 * 1024 * 1024
        ),
        name="tail",
    )(attended, residual, gain, lengths, wanted, weight, queue)


def body(
    queries, keys, values, residual, out_weight, norm_gain, source_queue, span_lengths, positives
):
    tok_rows = queries.shape[1]
    model_width = queries.shape[2]
    head_count = HEADS
    head_size = model_width // head_count
    reach_back = (WINDOW - 1) // tok_rows + 1
    seq_index = lax.axis_index("seq")
    first_pos = seq_index * tok_rows
    own_pair = jnp.stack([keys[0], values[0]])
    earlier = []
    for hop_count in range(1, reach_back + 1):
        earlier.append(shifted(own_pair, "seq", hop_count))
    ordered = earlier[::-1] + [own_pair]
    keys_all = jnp.concatenate([item[0] for item in ordered], axis=0)
    values_all = jnp.concatenate([item[1] for item in ordered], axis=0)
    query_pos = first_pos + jnp.arange(tok_rows, dtype=jnp.int32)
    key_pos = (
        first_pos - reach_back * tok_rows + jnp.arange((reach_back + 1) * tok_rows, dtype=jnp.int32)
    )
    distance = query_pos[:, None] - key_pos[None, :]
    allowed = (distance >= 0) & (distance < WINDOW) & (key_pos[None, :] >= 0)
    group_size = 4
    group_cols = group_size * head_size
    key_rows = keys_all.shape[0]

    def attend_group(group_index):
        first_col = group_index * group_cols
        query_group = lax.dynamic_slice_in_dim(queries[0], first_col, group_cols, 1).reshape(
            tok_rows, group_size, head_size
        )
        key_group = lax.dynamic_slice_in_dim(keys_all, first_col, group_cols, 1).reshape(
            key_rows, group_size, head_size
        )
        value_group = lax.dynamic_slice_in_dim(values_all, first_col, group_cols, 1).reshape(
            key_rows, group_size, head_size
        )
        scores = jnp.einsum(
            "qhd,khd->hqk", query_group, key_group, preferred_element_type=jnp.float32
        ) / math.sqrt(head_size)
        scores = jnp.where(allowed[None], scores, -jnp.inf)
        row_peak = jnp.max(scores, axis=-1, keepdims=True)
        exp_scores = jnp.exp(scores - row_peak)
        weights = (exp_scores / jnp.sum(exp_scores, axis=-1, keepdims=True)).astype(jnp.bfloat16)
        mixed = jnp.einsum("hqk,khd->qhd", weights, value_group, preferred_element_type=jnp.float32)
        return mixed.astype(jnp.bfloat16).reshape(tok_rows, group_cols)

    blocks = lax.map(attend_group, jnp.arange(head_count // group_size, dtype=jnp.int32))
    attended = jnp.transpose(blocks, (1, 0, 2)).reshape(tok_rows, model_width)
    own_rows = positives.shape[1]
    anchors, losses = tail(
        lax.axis_size("seq"),
        lax.axis_size("batch"),
        attended,
        residual[0],
        norm_gain.reshape(1, -1),
        span_lengths,
        positives.reshape(1, -1),
        out_weight,
        source_queue,
        own_rows,
    )
    return (anchors[None], losses[:, 0][None])


def solution(mesh):
    return jax.shard_map(
        body,
        mesh=mesh,
        in_specs=(
            P("batch", "seq", None),
            P("batch", "seq", None),
            P("batch", "seq", None),
            P("batch", "seq", None),
            P(),
            P(),
            P("batch", None),
            P("batch", None),
            P(None, "seq"),
        ),
        out_specs=(P("batch", "seq", None), P("batch", "seq")),
        check_vma=False,
    )
```

time: 196 us -> 155 us (0.79)
  waiting for transfers between devices: 90.7 us -> 37.9 us
  Pallas kernels: 0 us -> 39.4 us
  between operations: 14.2 us -> 0.76 us
  starting transfers between devices: 21.4 us -> 10.5 us
  blocking collectives: 9.26 us -> 0 us
  local copies, waits for them, and re-layouts: 22.7 us -> 27.5 us
    reduce_scatter x1 -> x0, waiting for transfers between devices: 43.5 us -> none  [body(): lax.psum_scatter(jnp.dot(member, normed, preferred_element_type=jnp.float...]
    pallas_call x0 -> x1, Pallas kernels: none -> 39.4 us  [tail(): pl.pallas_call(functools.partial(tail_kernel, n_seq, n_batch), out_shape=...]
    all_to_all x3 -> x0, waiting for transfers between devices: 10.6 us -> none  [the longest x1 4.6 us: body(): lax.all_to_all(positive.reshape(-1, own_rows), 'batch', split_axis=0, con...]
    all_to_all x3 -> x0, starting transfers between devices: 9.89 us -> none  [the longest x1 3.33 us: body(): lax.all_to_all(row_total.reshape(-1, own_rows), 'batch', split_axis=0, co...]
    all_gather x1 -> x0, blocking collectives: 9.26 us -> none  [body(): lax.all_gather(anchors, 'batch', axis=0, tiled=True)]
    and x4, other arithmetic: 1.09 us -> 6.49 us  [body(): allowed = (distance >= 0) & (distance < WINDOW) & (key_pos[None, :] >= 0)]
    sub x4, matrix products: 11.5 us -> 15.4 us  [attend_group(): exp_scores = jnp.exp(scores - row_peak)]
    dot_general x3 -> x0, matrix products: 3.69 us -> none  [the longest x1 2.11 us: body(): jnp.dot(attended, out_weight, preferred_element_type=jnp.float32)]
  transfers between devices with their start and end apart: 6 -> 2, of which waited for: 6 -> 2; matrix products, arithmetic and copies ran while one was open for 3% -> 2% of each run, Pallas kernels for 0% -> 0%
where the time goes in v1:
time: 155 us; the launch traced here: 154 us
  Pallas kernels  39.4 us (25%)
  waiting for transfers between devices  37.9 us (24%)
  local copies, waits for them, and re-layouts  27.5 us (18%)
  matrix products  25.7 us (17%)
  starting transfers between devices  10.5 us (7%)
  other arithmetic  9.55 us (6%)
  loops' own time  2.63 us (2%)
    pallas_call x1, Pallas kernels, tail(): pl.pallas_call(functools.partial(tail_kernel, n_seq, n_batch), out_shape=...  39.4 us
    ppermute x2, waiting for transfers between devices, shifted(): return lax.ppermute(array, axis, pairs)  37.9 us
    sub x4, matrix products, attend_group(): exp_scores = jnp.exp(scores - row_peak)  15.4 us
    ppermute x2, starting transfers between devices, shifted(): return lax.ppermute(array, axis, pairs)  10.5 us
    dot_general x4, matrix products, attend_group(): jnp.einsum('hqk,khd->qhd', weights, value_group, preferred_element_type=j...  10.3 us
    dynamic_slice x8, local copies, waits for them, and re-layouts, attend_group(): lax.dynamic_slice_in_dim(queries[0], first_col, group_cols, 1)  6.7 us
    and x4, other arithmetic, body(): allowed = (distance >= 0) & (distance < WINDOW) & (key_pos[None, :] >= 0)  6.49 us
    dynamic_slice x4, local copies, waits for them, and re-layouts, body(): lax.map(attend_group, jnp.arange(head_count // group_size, dtype=jnp.int32))  5.25 us
  transfers between devices with their start and end apart: 2, of which 2 were waited for; matrix products, arithmetic and copies ran while one was open for 2% of the time, Pallas kernels for 0%

profile of v1, /device:TPU:0, one launch (start us, length us, event | category | flops | bytes accessed | tf_op | source)
XLA Modules:
  0.0 153.9 jit_solution(4281328051719579403)
XLA Ops:
  3.2 6.9 %collective-permute-start = (bf16[2,256,1024]{1,2,0:T(8,128)(2,1)S(1)}, bf16[2,256,1024]{1,2,0:T(8,128)(2,1)}, u32[]{:S(2)}, u32[]{:S(2)}) collective-permute-start(bf16[2,256,1024]{1,2,0:T(8,128)(2,1)S(1)} %pad_maximum_fusion.2), channel_id=1, source_target_pairs={{0,16},{8,24},{1,17},{9,25},{2,18},{10,26},{3,19},{11,27},{4,20},{... | collective-permute-start | bytes 3145736 | tf_op jit(solution)/shard_map/ppermute | solution.py:24
  10.2 3.5 %collective-permute-start.1 = (bf16[2,256,1024]{1,2,0:T(8,128)(2,1)S(1)}, bf16[2,256,1024]{1,2,0:T(8,128)(2,1)S(1)}, u32[]{:S(2)}, u32[]{:S(2)}) collective-permute-start(bf16[2,256,1024]{1,2,0:T(8,128)(2,1)S(1)} %pad_maximum_fusion.2), channel_id=1, source_target_pairs={{0,8},{8,16},{16,24},{1,9},{9,17},{17,25},{2,10},{10,18},{18,26},{... | collective-permute-start | bytes 3145736 | tf_op jit(solution)/shard_map/ppermute | solution.py:24
  15.0 17.8 %collective-permute-done = bf16[2,256,1024]{1,2,0:T(8,128)(2,1)} collective-permute-done((bf16[2,256,1024]{1,2,0:T(8,128)(2,1)S(1)}, bf16[2,256,1024]{1,2,0:T(8,128)(2,1)}, u32[]{:S(2)}, u32[]{:S(2)}) %collective-permute-start) | collective-permute-done | bytes 1048608 | tf_op jit(solution)/shard_map/ppermute | solution.py:24
  32.8 1.3 slice_bitcast_fusion.1
  34.1 20.1 %collective-permute-done.1 = bf16[2,256,1024]{1,2,0:T(8,128)(2,1)S(1)} collective-permute-done((bf16[2,256,1024]{1,2,0:T(8,128)(2,1)S(1)}, bf16[2,256,1024]{1,2,0:T(8,128)(2,1)S(1)}, u32[]{:S(2)}, u32[]{:S(2)}) %collective-permute-start.1) | collective-permute-done | bytes 1048608 | tf_op jit(solution)/shard_map/ppermute | solution.py:24
  54.2 1.8 %pad_maximum_fusion = (bf16[768,1024]{0,1:T(8,128)(2,1)}, bf16[768,1024]{0,1:T(8,128)(2,1)}) fusion(bf16[256,1024]{0,1:T(8,128)(2,1)S(1)} %bitcast.51, bf16[256,1024]{0,1:T(8,128)(2,1)S(1)} %get-tuple-element.110, bf16[256,1024]{0,1:T(8,128)(2,1)S(1)} %get-tuple-element.108, bf16[256,1024]{0,1:T(8,128)(2,1)S(1)} %bitcast.50, ...), kind=kLoop, calls=%fused_computation.22 | loop fusion | flops 9437184 | bytes 6291456 | tf_op jit(solution)/shard_map/concatenate | solution.py:230
  56.6 54.1 %while.11 = (s32[]{:T(128)}, bf16[4,256,256]{1,2,0:T(8,128)(2,1)}, s32[4]{0:T(128)}, bf16[768,1024]{0,1:T(8,128)(2,1)}, bf16[1,256,1024]{2,1,0:T(8,128)(2,1)}, /...) while((s32[]{:T(128)}, bf16[4,256,256]{1,2,0:T(8,128)(2,1)}, ...), condition=%wide.region_3.4_spmd.clone, body=%wide.region_0.3_spmd.clone.sunk | while | flops 207094528 | bytes 10106303 | solution.py:262
  56.6 1.4 dynamic_slice.25
  61.6 1.6 %fusion.30 = pred[256,768]{1,0:T(8,128)(4,1)} fusion(s32[768]{0:T(1024)S(1)} %get-tuple-element.208, s32[256]{0:T(256)} %get-tuple-element.209, pred[768]{0:T(1024)(128)(4,1)} %get-tuple-element.210), kind=kLoop, calls=%fused_computation.14.clone.1 | loop fusion | flops 983040 | bytes 201472 | tf_op jit(solution)/shard_map/and | solution.py:236
  63.2 3.8 %fusion.31 = (f32[4,256]{1,0:T(4,128)S(1)}, f32[4,256,768]{2,1,0:T(8,128)}) fusion(pred[256,768]{1,0:T(8,128)(4,1)} %fusion.30, bf16[256,4,64]{0,2,1:T(8,128)(2,1)} %bitcast.52, bf16[768,4,64]{0,2,1:T(8,128)(2,1)S(1)} %bitcast.49), kind=kOutput, calls=%fused_computation.33.clone.1 | convolution fusion | flops 103809792 | bytes 3870720 | tf_op jit(solution)/shard_map/while/body/eval_jaxpr/sub | solution.py:257
  67.0 2.6 %fusion.32 = bf16[4,64,256]{2,1,0:T(8,128)(2,1)S(1)} fusion(bf16[768,4,64]{0,2,1:T(8,128)(2,1)S(1)} %bitcast.48, f32[4,256,768]{2,1,0:T(8,128)} %get-tuple-element.174, f32[4,256]{1,0:T(4,128)S(1)} %get-tuple-element.175), kind=kOutput, calls=%fused_computation.10.clone.1 | convolution fusion | flops 102301696 | bytes 3674112 | tf_op jit(solution)/shard_map/while/body/eval_jaxpr/hqk,khd->qhd/dot_general | solution.py:259
  70.3 1.3 dynamic_slice.25
  75.1 1.6 %fusion.30 = pred[256,768]{1,0:T(8,128)(4,1)} fusion(s32[768]{0:T(1024)S(1)} %get-tuple-element.208, s32[256]{0:T(256)} %get-tuple-element.209, pred[768]{0:T(1024)(128)(4,1)} %get-tuple-element.210), kind=kLoop, calls=%fused_computation.14.clone.1 | loop fusion | flops 983040 | bytes 201472 | tf_op jit(solution)/shard_map/and | solution.py:236
  76.7 3.8 %fusion.31 = (f32[4,256]{1,0:T(4,128)S(1)}, f32[4,256,768]{2,1,0:T(8,128)}) fusion(pred[256,768]{1,0:T(8,128)(4,1)} %fusion.30, bf16[256,4,64]{0,2,1:T(8,128)(2,1)} %bitcast.52, bf16[768,4,64]{0,2,1:T(8,128)(2,1)S(1)} %bitcast.49), kind=kOutput, calls=%fused_computation.33.clone.1 | convolution fusion | flops 103809792 | bytes 3870720 | tf_op jit(solution)/shard_map/while/body/eval_jaxpr/sub | solution.py:257
  80.5 2.6 %fusion.32 = bf16[4,64,256]{2,1,0:T(8,128)(2,1)S(1)} fusion(bf16[768,4,64]{0,2,1:T(8,128)(2,1)S(1)} %bitcast.48, f32[4,256,768]{2,1,0:T(8,128)} %get-tuple-element.174, f32[4,256]{1,0:T(4,128)S(1)} %get-tuple-element.175), kind=kOutput, calls=%fused_computation.10.clone.1 | convolution fusion | flops 102301696 | bytes 3674112 | tf_op jit(solution)/shard_map/while/body/eval_jaxpr/hqk,khd->qhd/dot_general | solution.py:259
  83.8 1.3 dynamic_slice.25
  88.5 1.6 %fusion.30 = pred[256,768]{1,0:T(8,128)(4,1)} fusion(s32[768]{0:T(1024)S(1)} %get-tuple-element.208, s32[256]{0:T(256)} %get-tuple-element.209, pred[768]{0:T(1024)(128)(4,1)} %get-tuple-element.210), kind=kLoop, calls=%fused_computation.14.clone.1 | loop fusion | flops 983040 | bytes 201472 | tf_op jit(solution)/shard_map/and | solution.py:236
  90.2 3.8 %fusion.31 = (f32[4,256]{1,0:T(4,128)S(1)}, f32[4,256,768]{2,1,0:T(8,128)}) fusion(pred[256,768]{1,0:T(8,128)(4,1)} %fusion.30, bf16[256,4,64]{0,2,1:T(8,128)(2,1)} %bitcast.52, bf16[768,4,64]{0,2,1:T(8,128)(2,1)S(1)} %bitcast.49), kind=kOutput, calls=%fused_computation.33.clone.1 | convolution fusion | flops 103809792 | bytes 3870720 | tf_op jit(solution)/shard_map/while/body/eval_jaxpr/sub | solution.py:257
  94.0 2.6 %fusion.32 = bf16[4,64,256]{2,1,0:T(8,128)(2,1)S(1)} fusion(bf16[768,4,64]{0,2,1:T(8,128)(2,1)S(1)} %bitcast.48, f32[4,256,768]{2,1,0:T(8,128)} %get-tuple-element.174, f32[4,256]{1,0:T(4,128)S(1)} %get-tuple-element.175), kind=kOutput, calls=%fused_computation.10.clone.1 | convolution fusion | flops 102301696 | bytes 3674112 | tf_op jit(solution)/shard_map/while/body/eval_jaxpr/hqk,khd->qhd/dot_general | solution.py:259
  97.2 1.3 dynamic_slice.25
  102.0 1.6 %fusion.30 = pred[256,768]{1,0:T(8,128)(4,1)} fusion(s32[768]{0:T(1024)S(1)} %get-tuple-element.208, s32[256]{0:T(256)} %get-tuple-element.209, pred[768]{0:T(1024)(128)(4,1)} %get-tuple-element.210), kind=kLoop, calls=%fused_computation.14.clone.1 | loop fusion | flops 983040 | bytes 201472 | tf_op jit(solution)/shard_map/and | solution.py:236
  103.6 3.8 %fusion.31 = (f32[4,256]{1,0:T(4,128)S(1)}, f32[4,256,768]{2,1,0:T(8,128)}) fusion(pred[256,768]{1,0:T(8,128)(4,1)} %fusion.30, bf16[256,4,64]{0,2,1:T(8,128)(2,1)} %bitcast.52, bf16[768,4,64]{0,2,1:T(8,128)(2,1)S(1)} %bitcast.49), kind=kOutput, calls=%fused_computation.33.clone.1 | convolution fusion | flops 103809792 | bytes 3870720 | tf_op jit(solution)/shard_map/while/body/eval_jaxpr/sub | solution.py:257
  107.5 2.6 %fusion.32 = bf16[4,64,256]{2,1,0:T(8,128)(2,1)S(1)} fusion(bf16[768,4,64]{0,2,1:T(8,128)(2,1)S(1)} %bitcast.48, f32[4,256,768]{2,1,0:T(8,128)} %get-tuple-element.174, f32[4,256]{1,0:T(4,128)S(1)} %get-tuple-element.175), kind=kOutput, calls=%fused_computation.10.clone.1 | convolution fusion | flops 102301696 | bytes 3674112 | tf_op jit(solution)/shard_map/while/body/eval_jaxpr/hqk,khd->qhd/dot_general | solution.py:259
  113.3 39.4 %tail.1 = (bf16[16,1024]{1,0:T(8,128)(2,1)S(1)}, f32[16,128]{1,0:T(8,128)S(1)}) custom-call(bf16[256,1024]{1,0:T(8,128)(2,1)S(1)} %copy.23.attended_ref, bf16[256,1024]{1,0:T(8,128)(2,1)S(1)} %bitcast.45, f32[1,1024]{1,0:T(1,128)S(1)} %bitcast.47, s32[1,64]{1,0:T(1,128)S(1)} %copy-done.4, s32[1,128]{1,0:T(1,128)S(1)} %reshape.45.wanted_ref, ...), custom_call_target="tpu_custom_call" | custom-call | tf_op jit(solution)/shard_map/tail/pallas_call | solution.py:184
  (41 shorter events, 22.2 us)
Async XLA Ops:
  0.6 13.1 %copy-start.5 = (s32[8,16]{1,0:T(8,128)S(1)}, s32[8,16]{1,0:T(8,128)}, u32[]{:S(2)}) copy-start(s32[8,16]{1,0:T(8,128)} %param.19) | copy-start | bytes 1540
  3.2 29.6 %collective-permute-start = (bf16[2,256,1024]{1,2,0:T(8,128)(2,1)S(1)}, bf16[2,256,1024]{1,2,0:T(8,128)(2,1)}, u32[]{:S(2)}, u32[]{:S(2)}) collective-permute-start(bf16[2,256,1024]{1,2,0:T(8,128)(2,1)S(1)} %pad_maximum_fusion.2), channel_id=1, source_target_pairs={{0,16},{8,24},{1,17},{9,25},{2,18},{10,26},{3,19},{11,27},{4,20},{... | collective-permute-start | bytes 3145736 | tf_op jit(solution)/shard_map/ppermute | solution.py:24
  10.2 43.9 %collective-permute-start.1 = (bf16[2,256,1024]{1,2,0:T(8,128)(2,1)S(1)}, bf16[2,256,1024]{1,2,0:T(8,128)(2,1)S(1)}, u32[]{:S(2)}, u32[]{:S(2)}) collective-permute-start(bf16[2,256,1024]{1,2,0:T(8,128)(2,1)S(1)} %pad_maximum_fusion.2), channel_id=1, source_target_pairs={{0,8},{8,16},{16,24},{1,9},{9,17},{17,25},{2,10},{10,18},{18,26},{... | collective-permute-start | bytes 3145736 | tf_op jit(solution)/shard_map/ppermute | solution.py:24
  56.6 55.4 %copy-start = (bf16[1024,1024]{1,0:T(8,128)(2,1)S(1)}, bf16[1024,1024]{1,0:T(8,128)(2,1)}, u32[]{:S(2)}) copy-start(bf16[1024,1024]{1,0:T(8,128)(2,1)} %weight_hbm.1) | copy-start | bytes 6291460
  56.6 55.4 %copy-start.2 = (bf16[1,256,1024]{2,1,0:T(8,128)(2,1)S(1)}, bf16[1,256,1024]{2,1,0:T(8,128)(2,1)}, u32[]{:S(2)}) copy-start(bf16[1,256,1024]{2,1,0:T(8,128)(2,1)} %param.14) | copy-start | bytes 1572868
  56.6 55.4 %copy-start.3 = (f32[1024]{0:T(1024)S(1)}, f32[1024]{0:T(1024)}, u32[]{:S(2)}) copy-start(f32[1024]{0:T(1024)} %param.16) | copy-start | bytes 12292
  56.6 55.4 %copy-start.4 = (s32[1,64]{1,0:T(1,128)S(1)}, s32[1,64]{1,0:T(1,128)}, u32[]{:S(2)}) copy-start(s32[1,64]{1,0:T(1,128)} %lengths_ref.1) | copy-start | bytes 772
  112.0 1.2 copy-start.1

commit v2 on v1

--- a/solution.py
+++ b/solution.py
@@ -18,31 +18,106 @@
 logit_scale = 20.0
 
 
-def shifted(array, axis, by):
-    devices = lax.axis_size(axis)
-    pairs = [(i, i + by) for i in range(devices) if 0 <= i + by < devices]
-    return lax.ppermute(array, axis, pairs)
-
-
-def tail_kernel(
+NEVER = -1e30
+
+
+def scores_to_partial(query_chunk, key_chunk, value_t, blocks_apart, head_size):
+    tok_rows, width = query_chunk.shape
+    lane = lax.broadcasted_iota(jnp.int32, (tok_rows, width), 1)
+    key_at = lax.broadcasted_iota(jnp.int32, (tok_rows, tok_rows), 0)
+    query_at = lax.broadcasted_iota(jnp.int32, (tok_rows, tok_rows), 1)
+    distance = blocks_apart * tok_rows + query_at - key_at
+    low = blocks_apart * tok_rows - (tok_rows - 1)
+    high = blocks_apart * tok_rows + tok_rows - 1
+    mixed, peaks, totals = [], [], []
+    for h in range(width // head_size):
+        own = (lane >= h * head_size) & (lane < (h + 1) * head_size)
+        query_h = jnp.where(own, query_chunk, jnp.zeros_like(query_chunk))
+        scores = lax.dot_general(
+            key_chunk, query_h, (((1,), (1,)), ((), ())), preferred_element_type=F32
+        ) * (1.0 / math.sqrt(head_size))
+        if low < 0:
+            scores = jnp.where(distance >= 0, scores, NEVER)
+        if high >= WINDOW:
+            scores = jnp.where(distance < WINDOW, scores, NEVER)
+        peak = jnp.max(scores, axis=0, keepdims=True)
+        weights = jnp.exp(scores - peak)
+        totals.append(jnp.sum(weights, axis=0, keepdims=True))
+        peaks.append(peak)
+        mixed.append(
+            jnp.dot(
+                value_t[h * head_size : (h + 1) * head_size, :],
+                weights.astype(BF16),
+                preferred_element_type=F32,
+            )
+        )
+    stats = jnp.concatenate(
+        peaks + totals + [jnp.zeros((8 - 2 * len(peaks), tok_rows), F32)], axis=0
+    )
+    return jnp.concatenate(mixed, axis=0), stats
+
+
+def merged(mixed_a, stats_a, mixed_b, stats_b, heads, head_size):
+    mixed, peaks, totals = [], [], []
+    for h in range(heads):
+        rows = slice(h * head_size, (h + 1) * head_size)
+        peak_a, peak_b = stats_a[h : h + 1], stats_b[h : h + 1]
+        peak = jnp.maximum(peak_a, peak_b)
+        keep_a, keep_b = jnp.exp(peak_a - peak), jnp.exp(peak_b - peak)
+        mixed.append(mixed_a[rows].astype(F32) * keep_a + mixed_b[rows].astype(F32) * keep_b)
+        totals.append(
+            stats_a[heads + h : heads + h + 1] * keep_a
+            + stats_b[heads + h : heads + h + 1] * keep_b
+        )
+        peaks.append(peak)
+    return mixed, peaks, totals
+
+
+def block_kernel(
     n_seq,
     n_batch,
-    attended_ref,
-    residual_ref,
+    head_size,
     gain_ref,
     lengths_ref,
     wanted_ref,
+    queries_hbm,
+    keys_hbm,
+    values_hbm,
+    residual_hbm,
     weight_hbm,
     queue_hbm,
     anchors_ref,
     losses_ref,
+    q_own,
+    k_own,
+    v_own,
+    v_t,
+    q_one,
+    q_two,
+    mix_own,
+    stat_own,
+    mix_one,
+    stat_one,
+    two_out,
+    two_out_stat,
+    two_in,
+    two_in_stat,
+    one_out,
+    one_out_stat,
+    one_in,
+    one_in_stat,
+    att_t,
+    residual,
     weight,
     queue,
     parts,
     parts_in,
     anchors_all,
     stats,
+    chunk_sem,
     load_sem,
+    send_sem,
+    recv_sem,
     part_send,
     part_recv,
     anchor_send,
@@ -50,12 +125,34 @@
     stat_send,
     stat_recv,
 ):
+    chunks, tok_rows, chunk_cols = q_own.shape
+    heads = chunk_cols // head_size
+    own_rows, width = anchors_ref.shape
+    funcs = own_rows * n_seq
     seq = lax.axis_index("seq")
     batch = lax.axis_index("batch")
-    weight_load = pltpu.make_async_copy(weight_hbm, weight, load_sem.at[0])
-    queue_load = pltpu.make_async_copy(queue_hbm, queue, load_sem.at[1])
+
+    def load(which, g):
+        source = (queries_hbm, keys_hbm, values_hbm)[which]
+        target = (q_own, k_own, v_own)[which]
+        cols = pl.ds(pl.multiple_of(g * chunk_cols, chunk_cols), chunk_cols)
+        return pltpu.make_async_copy(
+            source.at[:, cols], target.at[g], chunk_sem.at[which, g]
+        )
+
+    def start_loads(g, carry):
+        for which in range(3):
+            load(which, g).start()
+        return carry
+
+    lax.fori_loop(0, chunks, start_loads, 0)
+    residual_load = pltpu.make_async_copy(residual_hbm, residual, load_sem.at[0])
+    weight_load = pltpu.make_async_copy(weight_hbm, weight, load_sem.at[1])
+    queue_load = pltpu.make_async_copy(queue_hbm, queue, load_sem.at[2])
+    residual_load.start()
     weight_load.start()
     queue_load.start()
+
     seq_peers = [lax.rem(seq + d, n_seq) for d in range(1, n_seq)]
     batch_peers = [lax.rem(batch + d, n_batch) for d in range(1, n_batch)]
     barrier = pltpu.get_barrier_semaphore()
@@ -63,13 +160,155 @@
         pl.semaphore_signal(barrier, inc=1, device_id={"seq": peer}, device_id_type=MESH)
     for peer in batch_peers:
         pl.semaphore_signal(barrier, inc=1, device_id={"batch": peer}, device_id_type=MESH)
-
-    tok_rows = attended_ref.shape[0]
-    own_rows, width = anchors_ref.shape
-    funcs = own_rows * n_seq
+    pl.semaphore_wait(barrier, n_seq - 1 + n_batch - 1)
+
+    left = lax.rem(seq + n_seq - 1, n_seq)
+    right = lax.rem(seq + 1, n_seq)
+    has_left = seq >= 1
+    has_right = seq <= n_seq - 2
+    has_right_two = seq <= n_seq - 3
+
+    def remote(kind, source, target, g, peer):
+        return pltpu.make_async_remote_copy(
+            src_ref=source.at[g],
+            dst_ref=target.at[g],
+            send_sem=send_sem.at[kind, g],
+            recv_sem=recv_sem.at[kind, g],
+            device_id={"seq": peer},
+            device_id_type=MESH,
+        )
+
+    def ask_one(g):
+        return remote(0, q_own, q_one, g, left)
+
+    def ask_two(g):
+        return remote(1, q_one, q_two, g, left)
+
+    def give_two(g):
+        return (
+            remote(2, two_out, two_in, g, right),
+            remote(3, two_out_stat, two_in_stat, g, right),
+        )
+
+    def give_one(g):
+        return (
+            remote(4, one_out, one_in, g, right),
+            remote(5, one_out_stat, one_in_stat, g, right),
+        )
+
+    ahead = min(3, chunks)
+    for g in range(ahead):
+        load(0, g).wait()
+
+        @pl.when(has_left)
+        def _():
+            ask_one(g).start()
+
+    def step(t, carry):
+        fresh = t < chunks
+
+        @pl.when(fresh & has_right)
+        def _():
+            ask_one(t).wait_recv()
+
+            @pl.when(has_left)
+            def _():
+                ask_two(t).start()
+
+        @pl.when(t + ahead < chunks)
+        def _():
+            load(0, t + ahead).wait()
+
+            @pl.when(has_left)
+            def _():
+                ask_one(t + ahead).start()
+
+        @pl.when(fresh)
+        def _():
+            load(1, t).wait()
+            load(2, t).wait()
+            v_t[t] = v_own[t].T
+
+        @pl.when((t >= 2) & (t < chunks + 2) & has_right_two)
+        def _():
+            g = t - 2
+            ask_two(g).wait_recv()
+            mixed, stat = scores_to_partial(q_two[g], k_own[g], v_t.at[g], 2, head_size)
+            two_out[g] = mixed.astype(BF16)
+            two_out_stat[g] = stat
+            for copy in give_two(g):
+                copy.start()
+
+        @pl.when((t >= 4) & (t < chunks + 4) & has_right)
+        def _():
+            g = t - 4
+
+            @pl.when(has_left)
+            def _():
+                for copy in give_two(g):
+                    copy.wait_recv()
+                mixed, peaks, totals = merged(
+                    mix_one[g], stat_one[g], two_in[g], two_in_stat[g], heads, head_size
+                )
+                one_out[g] = jnp.concatenate(mixed, axis=0).astype(BF16)
+                one_out_stat[g] = jnp.concatenate(
+                    peaks + totals + [jnp.zeros((8 - 2 * heads, tok_rows), F32)], axis=0
+                )
+
+            @pl.when(jnp.logical_not(has_left))
+            def _():
+                one_out[g] = mix_one[g].astype(BF16)
+                one_out_stat[g] = stat_one[g]
+
+            for copy in give_one(g):
+                copy.start()
+
+        @pl.when(fresh)
+        def _():
+            mixed, stat = scores_to_partial(q_own[t], k_own[t], v_t.at[t], 0, head_size)
+            mix_own[t] = mixed
+            stat_own[t] = stat
+
+        @pl.when(fresh & has_right)
+        def _():
+            mixed, stat = scores_to_partial(q_one[t], k_own[t], v_t.at[t], 1, head_size)
+            mix_one[t] = mixed
+            stat_one[t] = stat
+
+        @pl.when((t >= 6) & (t < chunks + 6))
+        def _():
+            g = t - 6
+
+            @pl.when(has_left)
+            def _():
+                for copy in give_one(g):
+                    copy.wait_recv()
+                mixed, peaks, totals = merged(
+                    mix_own[g], stat_own[g], one_in[g], one_in_stat[g], heads, head_size
+                )
+                att_t[g] = jnp.concatenate(
+                    [m / l for m, l in zip(mixed, totals)], axis=0
+                ).astype(BF16)
+
+            @pl.when(jnp.logical_not(has_left))
+            def _():
+                for h in range(heads):
+                    rows = slice(h * head_size, (h + 1) * head_size)
+                    att_t[g, rows, :] = (
+                        mix_own[g, rows, :] / stat_own[g, heads + h : heads + h + 1, :]
+                    ).astype(BF16)
+
+        return carry
+
+    lax.fori_loop(0, chunks + 6, step, 0)
+
+    residual_load.wait()
     weight_load.wait()
-    hidden = residual_ref[...].astype(F32) + jnp.dot(
-        attended_ref[...], weight[...], preferred_element_type=F32
+    hidden = residual[...].astype(F32) + lax.dot_general(
+        att_t[...].reshape(width, tok_rows),
+        weight[...],
+        (((0,), (0,)), ((), ())),
+        preferred_element_type=F32,
     )
     scale = lax.rsqrt(jnp.mean(hidden * hidden, axis=-1, keepdims=True) + 1e-05)
     normed = (hidden * scale * gain_ref[...]).astype(BF16)
@@ -87,7 +326,6 @@
     partial = jnp.dot(member, normed, preferred_element_type=F32)
     parts[...] = partial.reshape(n_seq, own_rows, width).astype(BF16)
 
-    pl.semaphore_wait(barrier, n_seq - 1 + n_batch - 1)
     copies = []
     for d in range(1, n_seq):
         copy = pltpu.make_async_remote_copy(
@@ -175,28 +413,87 @@
     )
     losses_ref[...] = jnp.broadcast_to(loss_col, losses_ref.shape)
 
-
-def tail(n_seq, n_batch, attended, residual, gain, lengths, wanted, weight, queue, own_rows):
-    width = attended.shape[1]
+    def drain(g, carry):
+        @pl.when(has_left)
+        def _():
+            ask_one(g).wait_send()
+
+            @pl.when(has_right)
+            def _():
+                ask_two(g).wait_send()
+
+        @pl.when(has_right_two)
+        def _():
+            for copy in give_two(g):
+                copy.wait_send()
+
+        @pl.when(has_right)
+        def _():
+            for copy in give_one(g):
+                copy.wait_send()
+
+        return carry
+
+    lax.fori_loop(0, chunks, drain, 0)
+
+
+def body(
+    queries, keys, values, residual, out_weight, norm_gain, source_queue, span_lengths, positives
+):
+    tok_rows, width = queries.shape[1:]
+    head_size = width // HEADS
+    n_seq = lax.axis_size("seq")
+    n_batch = lax.axis_size("batch")
+    own_rows = positives.shape[1]
     rows = n_batch * own_rows
+    chunk_cols = 128
+    chunks = width // chunk_cols
+    assert (WINDOW - 1) // tok_rows + 1 == 2 and chunk_cols % head_size == 0
     vmem = pl.BlockSpec(memory_space=pltpu.VMEM)
     hbm = pl.BlockSpec(memory_space=pl.ANY)
-    return pl.pallas_call(
-        functools.partial(tail_kernel, n_seq, n_batch),
+    rows_bf16 = pltpu.VMEM((chunks, tok_rows, chunk_cols), BF16)
+    cols_bf16 = pltpu.VMEM((chunks, chunk_cols, tok_rows), BF16)
+    cols_f32 = pltpu.VMEM((chunks, chunk_cols, tok_rows), F32)
+    stat_f32 = pltpu.VMEM((chunks, 8, tok_rows), F32)
+    anchors, losses = pl.pallas_call(
+        functools.partial(block_kernel, n_seq, n_batch, head_size),
         out_shape=(
             jax.ShapeDtypeStruct((own_rows, width), BF16),
             jax.ShapeDtypeStruct((own_rows, 128), F32),
         ),
-        in_specs=[vmem] * 5 + [hbm] * 2,
+        in_specs=[vmem] * 3 + [hbm] * 6,
         out_specs=(vmem, vmem),
         scratch_shapes=[
-            pltpu.VMEM(weight.shape, BF16),
-            pltpu.VMEM(queue.shape, BF16),
+            rows_bf16,
+            rows_bf16,
+            rows_bf16,
+            cols_bf16,
+            rows_bf16,
+            rows_bf16,
+            cols_f32,
+            stat_f32,
+            cols_f32,
+            stat_f32,
+            cols_bf16,
+            stat_f32,
+            cols_bf16,
+            stat_f32,
+            cols_bf16,
+            stat_f32,
+            cols_bf16,
+            stat_f32,
+            cols_bf16,
+            pltpu.VMEM((tok_rows, width), BF16),
+            pltpu.VMEM(out_weight.shape, BF16),
+            pltpu.VMEM(source_queue.shape, BF16),
             pltpu.VMEM((n_seq, own_rows, width), BF16),
             pltpu.VMEM((n_seq - 1, own_rows, width), BF16),
             pltpu.VMEM((n_batch, own_rows, width), BF16),
             pltpu.VMEM((n_batch, 8, rows), F32),
-            pltpu.SemaphoreType.DMA((2,)),
+            pltpu.SemaphoreType.DMA((3, chunks)),
+            pltpu.SemaphoreType.DMA((3,)),
+            pltpu.SemaphoreType.DMA((6, chunks)),
+            pltpu.SemaphoreType.DMA((6, chunks)),
             pltpu.SemaphoreType.DMA((n_seq - 1,)),
             pltpu.SemaphoreType.DMA((n_seq - 1,)),
             pltpu.SemaphoreType.DMA((n_batch - 1,)),
@@ -205,74 +502,19 @@
             pltpu.SemaphoreType.DMA((n_batch - 1,)),
         ],
         compiler_params=pltpu.CompilerParams(
-            collective_id=0, has_side_effects=True, vmem_limit_bytes=40 * 1024 * 1024
+            collective_id=0, has_side_effects=True, vmem_limit_bytes=48 * 1024 * 1024
         ),
-        name="tail",
-    )(attended, residual, gain, lengths, wanted, weight, queue)
-
-
-def body(
-    queries, keys, values, residual, out_weight, norm_gain, source_queue, span_lengths, positives
-):
-    tok_rows = queries.shape[1]
-    model_width = queries.shape[2]
-    head_count = HEADS
-    head_size = model_width // head_count
-    reach_back = (WINDOW - 1) // tok_rows + 1
-    seq_index = lax.axis_index("seq")
-    first_pos = seq_index * tok_rows
-    own_pair = jnp.stack([keys[0], values[0]])
-    earlier = []
-    for hop_count in range(1, reach_back + 1):
-        earlier.append(shifted(own_pair, "seq", hop_count))
-    ordered = earlier[::-1] + [own_pair]
-    keys_all = jnp.concatenate([item[0] for item in ordered], axis=0)
-    values_all = jnp.concatenate([item[1] for item in ordered], axis=0)
-    query_pos = first_pos + jnp.arange(tok_rows, dtype=jnp.int32)
-    key_pos = (
-        first_pos - reach_back * tok_rows + jnp.arange((reach_back + 1) * tok_rows, dtype=jnp.int32)
-    )
-    distance = query_pos[:, None] - key_pos[None, :]
-    allowed = (distance >= 0) & (distance < WINDOW) & (key_pos[None, :] >= 0)
-    group_size = 4
-    group_cols = group_size * head_size
-    key_rows = keys_all.shape[0]
-
-    def attend_group(group_index):
-        first_col = group_index * group_cols
-        query_group = lax.dynamic_slice_in_dim(queries[0], first_col, group_cols, 1).reshape(
-            tok_rows, group_size, head_size
-        )
-        key_group = lax.dynamic_slice_in_dim(keys_all, first_col, group_cols, 1).reshape(
-            key_rows, group_size, head_size
-        )
-        value_group = lax.dynamic_slice_in_dim(values_all, first_col, group_cols, 1).reshape(
-            key_rows, group_size, head_size
-        )
-        scores = jnp.einsum(
-            "qhd,khd->hqk", query_group, key_group, preferred_element_type=jnp.float32
-        ) / math.sqrt(head_size)
-        scores = jnp.where(allowed[None], scores, -jnp.inf)
-        row_peak = jnp.max(scores, axis=-1, keepdims=True)
-        exp_scores = jnp.exp(scores - row_peak)
-        weights = (exp_scores / jnp.sum(exp_scores, axis=-1, keepdims=True)).astype(jnp.bfloat16)
-        mixed = jnp.einsum("hqk,khd->qhd", weights, value_group, preferred_element_type=jnp.float32)
-        return mixed.astype(jnp.bfloat16).reshape(tok_rows, group_cols)
-
-    blocks = lax.map(attend_group, jnp.arange(head_count // group_size, dtype=jnp.int32))
-    attended = jnp.transpose(blocks, (1, 0, 2)).reshape(tok_rows, model_width)
-    own_rows = positives.shape[1]
-    anchors, losses = tail(
-        lax.axis_size("seq"),
-        lax.axis_size("batch"),
-        attended,
-        residual[0],
+        name="block",
+    )(
         norm_gain.reshape(1, -1),
         span_lengths,
         positives.reshape(1, -1),
+        queries[0],
+        keys[0],
+        values[0],
+        residual[0],
         out_weight,
         source_queue,
-        own_rows,
     )
     return (anchors[None], losses[:, 0][None])
 

time: 155 us -> 69.9 us (0.45)
  waiting for transfers between devices: 37.9 us -> 0 us
  matrix products: 25.7 us -> 0 us
  Pallas kernels: 39.4 us -> 58.5 us
  local copies, waits for them, and re-layouts: 27.5 us -> 10.3 us
  starting transfers between devices: 10.5 us -> 0 us
  other arithmetic: 9.55 us -> 0 us
  loops' own time: 2.63 us -> 0 us
    ppermute x2 -> x0, waiting for transfers between devices: 37.9 us -> none  [shifted(): return lax.ppermute(array, axis, pairs)]
    pallas_call x1, Pallas kernels: 39.4 us -> 58.5 us  [body(): pl.pallas_call(functools.partial(block_kernel, n_seq, n_batch, head_size)...]
    dynamic_slice x16 -> x0, local copies, waits for them, and re-layouts: 16.6 us -> none  [the longest x8 6.7 us: attend_group(): lax.dynamic_slice_in_dim(queries[0], first_col, group_cols, 1)]
    sub x4 -> x0, matrix products: 15.4 us -> none  [attend_group(): exp_scores = jnp.exp(scores - row_peak)]
    ppermute x2 -> x0, starting transfers between devices: 10.5 us -> none  [shifted(): return lax.ppermute(array, axis, pairs)]
    dot_general x4 -> x0, matrix products: 10.3 us -> none  [attend_group(): jnp.einsum('hqk,khd->qhd', weights, value_group, preferred_element_type=j...]
    and x4 -> x0, other arithmetic: 6.49 us -> none  [body(): allowed = (distance >= 0) & (distance < WINDOW) & (key_pos[None, :] >= 0)]
    unnamed x15 -> x17, local copies, waits for them, and re-layouts: 4.35 us -> 8.94 us
  transfers between devices with their start and end apart: 2 -> 0, of which waited for: 2 -> 0; matrix products, arithmetic and copies ran while one was open for 2% -> 0% of each run, Pallas kernels for 0% -> 0%
where the time goes in v2:
time: 69.9 us; the launch traced here: 69.4 us
  Pallas kernels  58.5 us (84%)
  local copies, waits for them, and re-layouts  10.3 us (15%)
    pallas_call x1, Pallas kernels, body(): pl.pallas_call(functools.partial(block_kernel, n_seq, n_batch, head_size)...  58.5 us
    unnamed x17, local copies, waits for them, and re-layouts  8.94 us

profile of v2, /device:TPU:0, one launch (start us, length us, event | category | flops | bytes accessed | tf_op | source)
XLA Modules:
  0.0 69.4 jit_solution(7166381459300975206)
XLA Ops:
  0.6 0.8 %reshape.11.wanted_ref = s32[1,128]{1,0:T(1,128)S(1)} reshape(s32[8,16]{1,0:T(8,128)} %param.17) | data formatting | bytes 1024 | tf_op jit(solution)/shard_map/reshape | solution.py:511
  1.4 0.0 copy-start
  1.4 1.6 %copy-done = bf16[1024,1024]{1,0:T(8,128)(2,1)S(1)} copy-done((bf16[1024,1024]{1,0:T(8,128)(2,1)S(1)}, bf16[1024,1024]{1,0:T(8,128)(2,1)}, u32[]{:S(2)}) %copy-start) | copy-done | bytes 2097176
  3.0 0.0 copy-start.1
  3.0 1.2 %copy-done.1 = bf16[512,1024]{1,0:T(8,128)(2,1)S(1)} copy-done((bf16[512,1024]{1,0:T(8,128)(2,1)S(1)}, bf16[512,1024]{1,0:T(8,128)(2,1)}, u32[]{:S(2)}) %copy-start.1) | copy-done | bytes 1048600
  4.2 0.0 copy-start.2
  4.2 1.0 %copy-done.2 = bf16[1,256,1024]{2,1,0:T(8,128)(2,1)S(1)} copy-done((bf16[1,256,1024]{2,1,0:T(8,128)(2,1)S(1)}, bf16[1,256,1024]{2,1,0:T(8,128)(2,1)}, u32[]{:S(2)}) %copy-start.2) | copy-done | bytes 524312
  5.3 0.0 copy-start.3
  5.3 1.0 %copy-done.3 = bf16[1,256,1024]{2,1,0:T(8,128)(2,1)S(1)} copy-done((bf16[1,256,1024]{2,1,0:T(8,128)(2,1)S(1)}, bf16[1,256,1024]{2,1,0:T(8,128)(2,1)}, u32[]{:S(2)}) %copy-start.3) | copy-done | bytes 524312
  6.3 0.0 copy-start.4
  6.3 1.0 %copy-done.4 = bf16[1,256,1024]{2,1,0:T(8,128)(2,1)S(1)} copy-done((bf16[1,256,1024]{2,1,0:T(8,128)(2,1)S(1)}, bf16[1,256,1024]{2,1,0:T(8,128)(2,1)}, u32[]{:S(2)}) %copy-start.4) | copy-done | bytes 524312
  7.3 0.0 copy-start.5
  7.3 1.0 %copy-done.5 = bf16[1,256,1024]{2,1,0:T(8,128)(2,1)S(1)} copy-done((bf16[1,256,1024]{2,1,0:T(8,128)(2,1)S(1)}, bf16[1,256,1024]{2,1,0:T(8,128)(2,1)}, u32[]{:S(2)}) %copy-start.5) | copy-done | bytes 524312
  8.4 0.0 copy-start.6
  8.4 0.7 copy-done.6
  9.1 0.0 copy-start.7
  9.1 0.7 copy-done.7
  9.7 58.5 %block.1 = (bf16[16,1024]{1,0:T(8,128)(2,1)S(1)}, f32[16,128]{1,0:T(8,128)S(1)}) custom-call(f32[1,1024]{1,0:T(1,128)S(1)} %bitcast.12, s32[1,64]{1,0:T(1,128)S(1)} %copy-done.7, s32[1,128]{1,0:T(1,128)S(1)} %reshape.11.wanted_ref, bf16[256,1024]{1,0:T(8,128)(2,1)S(1)} %bitcast.7, bf16[256,1024]{1,0:T(8,128)(2,1)S(1)} %bitcast.8, ...), custom_call_target="tpu_custom_call" | custom-call | tf_op jit(solution)/shard_map/block/pallas_call | solution.py:458
  68.2 0.6 slice_reduce_fusion
  68.8 0.6 copy.12
Async XLA Ops:
  1.4 1.6 %copy-start = (bf16[1024,1024]{1,0:T(8,128)(2,1)S(1)}, bf16[1024,1024]{1,0:T(8,128)(2,1)}, u32[]{:S(2)}) copy-start(bf16[1024,1024]{1,0:T(8,128)(2,1)} %weight_hbm.1) | copy-start | bytes 6291460
  3.0 1.2 %copy-start.1 = (bf16[512,1024]{1,0:T(8,128)(2,1)S(1)}, bf16[512,1024]{1,0:T(8,128)(2,1)}, u32[]{:S(2)}) copy-start(bf16[512,1024]{1,0:T(8,128)(2,1)} %queue_hbm.1) | copy-start | bytes 3145732
  4.2 1.0 %copy-start.2 = (bf16[1,256,1024]{2,1,0:T(8,128)(2,1)S(1)}, bf16[1,256,1024]{2,1,0:T(8,128)(2,1)}, u32[]{:S(2)}) copy-start(bf16[1,256,1024]{2,1,0:T(8,128)(2,1)} %param.9) | copy-start | bytes 1572868
  5.3 1.0 %copy-start.3 = (bf16[1,256,1024]{2,1,0:T(8,128)(2,1)S(1)}, bf16[1,256,1024]{2,1,0:T(8,128)(2,1)}, u32[]{:S(2)}) copy-start(bf16[1,256,1024]{2,1,0:T(8,128)(2,1)} %param.10) | copy-start | bytes 1572868
  6.3 1.0 %copy-start.4 = (bf16[1,256,1024]{2,1,0:T(8,128)(2,1)S(1)}, bf16[1,256,1024]{2,1,0:T(8,128)(2,1)}, u32[]{:S(2)}) copy-start(bf16[1,256,1024]{2,1,0:T(8,128)(2,1)} %param.11) | copy-start | bytes 1572868
  7.3 1.0 %copy-start.5 = (bf16[1,256,1024]{2,1,0:T(8,128)(2,1)S(1)}, bf16[1,256,1024]{2,1,0:T(8,128)(2,1)}, u32[]{:S(2)}) copy-start(bf16[1,256,1024]{2,1,0:T(8,128)(2,1)} %param.12) | copy-start | bytes 1572868
  8.4 0.7 copy-start.6
  9.1 0.7 copy-start.7

commit v3 on v2

--- a/solution.py
+++ b/solution.py
@@ -21,36 +21,53 @@
 NEVER = -1e30
 
 
-def scores_to_partial(query_chunk, key_chunk, value_t, blocks_apart, head_size):
+def scores_to_partial(query_chunk, key_ref, value_t, blocks_apart, head_size):
     tok_rows, width = query_chunk.shape
+    half = tok_rows // 2
+    to_log2 = math.log2(math.e) / math.sqrt(head_size)
     lane = lax.broadcasted_iota(jnp.int32, (tok_rows, width), 1)
-    key_at = lax.broadcasted_iota(jnp.int32, (tok_rows, tok_rows), 0)
-    query_at = lax.broadcasted_iota(jnp.int32, (tok_rows, tok_rows), 1)
-    distance = blocks_apart * tok_rows + query_at - key_at
-    low = blocks_apart * tok_rows - (tok_rows - 1)
-    high = blocks_apart * tok_rows + tok_rows - 1
+    query_less_key = lax.broadcasted_iota(jnp.int32, (half, half), 1) - lax.broadcasted_iota(
+        jnp.int32, (half, half), 0
+    )
     mixed, peaks, totals = [], [], []
     for h in range(width // head_size):
         own = (lane >= h * head_size) & (lane < (h + 1) * head_size)
         query_h = jnp.where(own, query_chunk, jnp.zeros_like(query_chunk))
-        scores = lax.dot_general(
-            key_chunk, query_h, (((1,), (1,)), ((), ())), preferred_element_type=F32
-        ) * (1.0 / math.sqrt(head_size))
-        if low < 0:
-            scores = jnp.where(distance >= 0, scores, NEVER)
-        if high >= WINDOW:
-            scores = jnp.where(distance < WINDOW, scores, NEVER)
-        peak = jnp.max(scores, axis=0, keepdims=True)
-        weights = jnp.exp(scores - peak)
-        totals.append(jnp.sum(weights, axis=0, keepdims=True))
-        peaks.append(peak)
-        mixed.append(
-            jnp.dot(
-                value_t[h * head_size : (h + 1) * head_size, :],
-                weights.astype(BF16),
+        mixed_h, peaks_h, totals_h = [], [], []
+        for i in range(2):
+            offsets = [blocks_apart * tok_rows + (i - j) * half for j in range(2)]
+            seen = [j for j in range(2) if -half < offsets[j] < WINDOW + half - 1]
+            first, last = seen[0] * half, (seen[-1] + 1) * half
+            scores = lax.dot_general(
+                key_ref[first:last, :],
+                query_h[i * half : (i + 1) * half],
+                (((1,), (1,)), ((), ())),
                 preferred_element_type=F32,
             )
-        )
+            parts = []
+            for j in seen:
+                part = scores[j * half - first : (j + 1) * half - first]
+                if offsets[j] < half - 1:
+                    part = jnp.where(query_less_key >= -offsets[j], part, NEVER)
+                if offsets[j] + half - 1 >= WINDOW:
+                    part = jnp.where(query_less_key < WINDOW - offsets[j], part, NEVER)
+                parts.append(part)
+            peak = functools.reduce(
+                jnp.maximum, [jnp.max(part, axis=0, keepdims=True) for part in parts]
+            )
+            parts = [jnp.exp2((part - peak) * to_log2) for part in parts]
+            totals_h.append(sum(jnp.sum(part, axis=0, keepdims=True) for part in parts))
+            peaks_h.append(peak)
+            mixed_h.append(
+                jnp.dot(
+                    value_t[h * head_size : (h + 1) * head_size, first:last],
+                    jnp.concatenate([part.astype(BF16) for part in parts], axis=0),
+                    preferred_element_type=F32,
+                )
+            )
+        mixed.append(jnp.concatenate(mixed_h, axis=1))
+        peaks.append(jnp.concatenate(peaks_h, axis=1))
+        totals.append(jnp.concatenate(totals_h, axis=1))
     stats = jnp.concatenate(
         peaks + totals + [jnp.zeros((8 - 2 * len(peaks), tok_rows), F32)], axis=0
     )
@@ -58,12 +75,14 @@
 
 
 def merged(mixed_a, stats_a, mixed_b, stats_b, heads, head_size):
+    to_log2 = math.log2(math.e) / math.sqrt(head_size)
     mixed, peaks, totals = [], [], []
     for h in range(heads):
         rows = slice(h * head_size, (h + 1) * head_size)
         peak_a, peak_b = stats_a[h : h + 1], stats_b[h : h + 1]
         peak = jnp.maximum(peak_a, peak_b)
-        keep_a, keep_b = jnp.exp(peak_a - peak), jnp.exp(peak_b - peak)
+        keep_a = jnp.exp2((peak_a - peak) * to_log2)
+        keep_b = jnp.exp2((peak_b - peak) * to_log2)
         mixed.append(mixed_a[rows].astype(F32) * keep_a + mixed_b[rows].astype(F32) * keep_b)
         totals.append(
             stats_a[heads + h : heads + h + 1] * keep_a
@@ -114,6 +133,7 @@
     parts_in,
     anchors_all,
     stats,
+    wanted,
     chunk_sem,
     load_sem,
     send_sem,
@@ -153,6 +173,21 @@
     weight_load.start()
     queue_load.start()
 
+    rows = n_batch * own_rows
+    spread_at = lax.broadcasted_iota(jnp.int32, (own_rows, rows), 1)
+    spread = (
+        lax.rem(spread_at, own_rows) == lax.broadcasted_iota(jnp.int32, (own_rows, rows), 0)
+    )
+    spread = jnp.where(spread, 1.0, 0.0).astype(BF16)
+    high = wanted_ref[...] // 128
+    low = wanted_ref[...] - high * 128
+    whole = 128.0 * jnp.dot(
+        high.astype(F32).astype(BF16), spread, preferred_element_type=F32
+    ) + jnp.dot(low.astype(F32).astype(BF16), spread, preferred_element_type=F32)
+    mine = lax.broadcasted_iota(jnp.int32, (n_batch, rows), 1) // own_rows
+    mine = mine == lax.broadcasted_iota(jnp.int32, (n_batch, rows), 0)
+    wanted[...] = jnp.sum(jnp.where(mine, whole, 0.0), axis=0, keepdims=True).astype(jnp.int32)
+
     seq_peers = [lax.rem(seq + d, n_seq) for d in range(1, n_seq)]
     batch_peers = [lax.rem(batch + d, n_batch) for d in range(1, n_batch)]
     barrier = pltpu.get_barrier_semaphore()
@@ -204,6 +239,20 @@
         def _():
             ask_one(g).start()
 
+    def attend_own(g):
+        load(1, g).wait()
+        load(2, g).wait()
+        v_t[g] = v_own[g].T
+        mixed, stat = scores_to_partial(q_own[g], k_own.at[g], v_t.at[g], 0, head_size)
+        mix_own[g] = mixed
+        stat_own[g] = stat
+
+    def attend_first(g, carry):
+        attend_own(g)
+        return carry
+
+    lax.fori_loop(0, ahead, attend_first, 0)
+
     def step(t, carry):
         fresh = t < chunks
 
@@ -223,17 +272,11 @@
             def _():
                 ask_one(t + ahead).start()
 
-        @pl.when(fresh)
-        def _():
-            load(1, t).wait()
-            load(2, t).wait()
-            v_t[t] = v_own[t].T
-
         @pl.when((t >= 2) & (t < chunks + 2) & has_right_two)
         def _():
             g = t - 2
             ask_two(g).wait_recv()
-            mixed, stat = scores_to_partial(q_two[g], k_own[g], v_t.at[g], 2, head_size)
+            mixed, stat = scores_to_partial(q_two[g], k_own.at[g], v_t.at[g], 2, head_size)
             two_out[g] = mixed.astype(BF16)
             two_out_stat[g] = stat
             for copy in give_two(g):
@@ -263,17 +306,15 @@
             for copy in give_one(g):
                 copy.start()
 
-        @pl.when(fresh)
-        def _():
-            mixed, stat = scores_to_partial(q_own[t], k_own[t], v_t.at[t], 0, head_size)
-            mix_own[t] = mixed
-            stat_own[t] = stat
-
         @pl.when(fresh & has_right)
         def _():
-            mixed, stat = scores_to_partial(q_one[t], k_own[t], v_t.at[t], 1, head_size)
+            mixed, stat = scores_to_partial(q_one[t], k_own.at[t], v_t.at[t], 1, head_size)
             mix_one[t] = mixed
             stat_one[t] = stat
+
+        @pl.when(t + ahead < chunks)
+        def _():
+            attend_own(t + ahead)
 
         @pl.when((t >= 6) & (t < chunks + 6))
         def _():
@@ -365,7 +406,6 @@
     queue_load.wait()
     for copy in copies:
         copy.wait()
-    rows = n_batch * own_rows
     logits = logit_scale * lax.dot_general(
         queue[...],
         anchors_all[...].reshape(rows, width),
@@ -377,7 +417,7 @@
     row_peak = jnp.max(logits, axis=0, keepdims=True)
     row_total = jnp.sum(jnp.exp(logits - row_peak), axis=0, keepdims=True)
     positive = jnp.sum(
-        jnp.where(wanted_ref[...] == queue_ids, logits, 0.0), axis=0, keepdims=True
+        jnp.where(wanted[...] == queue_ids, logits, 0.0), axis=0, keepdims=True
     )
     stats[batch] = jnp.concatenate(
         [row_peak, row_total, positive, jnp.zeros((5, rows), F32)], axis=0
@@ -411,7 +451,13 @@
         axis=1,
         keepdims=True,
     )
-    losses_ref[...] = jnp.broadcast_to(loss_col, losses_ref.shape)
+    square = (own_rows, own_rows)
+    diagonal = lax.broadcasted_iota(jnp.int32, square, 0) == lax.broadcasted_iota(
+        jnp.int32, square, 1
+    )
+    losses_ref[...] = jnp.sum(
+        jnp.where(diagonal, jnp.broadcast_to(loss_col, square), 0.0), axis=0, keepdims=True
+    )
 
     def drain(g, carry):
         @pl.when(has_left)
@@ -459,7 +505,7 @@
         functools.partial(block_kernel, n_seq, n_batch, head_size),
         out_shape=(
             jax.ShapeDtypeStruct((own_rows, width), BF16),
-            jax.ShapeDtypeStruct((own_rows, 128), F32),
+            jax.ShapeDtypeStruct((1, own_rows), F32),
         ),
         in_specs=[vmem] * 3 + [hbm] * 6,
         out_specs=(vmem, vmem),
@@ -490,6 +536,7 @@
             pltpu.VMEM((n_seq - 1, own_rows, width), BF16),
             pltpu.VMEM((n_batch, own_rows, width), BF16),
             pltpu.VMEM((n_batch, 8, rows), F32),
+            pltpu.VMEM((1, rows), jnp.int32),
             pltpu.SemaphoreType.DMA((3, chunks)),
             pltpu.SemaphoreType.DMA((3,)),
             pltpu.SemaphoreType.DMA((6, chunks)),
@@ -502,13 +549,13 @@
             pltpu.SemaphoreType.DMA((n_batch - 1,)),
         ],
         compiler_params=pltpu.CompilerParams(
-            collective_id=0, has_side_effects=True, vmem_limit_bytes=48 * 1024 * 1024
+            collective_id=0, has_side_effects=True, vmem_limit_bytes=67043328
         ),
         name="block",
     )(
         norm_gain.reshape(1, -1),
         span_lengths,
-        positives.reshape(1, -1),
+        positives,
         queries[0],
         keys[0],
         values[0],
@@ -516,7 +563,7 @@
         out_weight,
         source_queue,
     )
-    return (anchors[None], losses[:, 0][None])
+    return (anchors[None], losses)
 
 
 def solution(mesh):

time: 69.9 us -> 62.8 us (0.90)
  local copies, waits for them, and re-layouts: 10.3 us -> 2.55 us
  Pallas kernels: 58.5 us -> 59.3 us
    unnamed x17 -> x2, local copies, waits for them, and re-layouts: 8.94 us -> 2.55 us
    pallas_call x1, Pallas kernels: 58.5 us -> 59.3 us  [body(): pl.pallas_call(functools.partial(block_kernel, n_seq, n_batch, head_size)...]
    reshape x1 -> x0, local copies, waits for them, and re-layouts: 0.77 us -> none  [body(): positives.reshape(1, -1)]
where the time goes in v3:
time: 62.8 us; the launch traced here: 62.5 us
  Pallas kernels  59.3 us (94%)
  local copies, waits for them, and re-layouts  2.55 us (4%)
  between operations  0.64 us (1%)
    pallas_call x1, Pallas kernels, body(): pl.pallas_call(functools.partial(block_kernel, n_seq, n_batch, head_size)...  59.3 us
    unnamed x2, local copies, waits for them, and re-layouts  2.55 us

profile of v3, /device:TPU:0, one launch (start us, length us, event | category | flops | bytes accessed | tf_op | source)
XLA Modules:
  0.0 62.5 jit_solution(8285732574012183756)
XLA Ops:
  0.6 59.3 %block.1 = (bf16[16,1024]{1,0:T(8,128)(2,1)}, f32[1,16]{1,0:T(1,128)}) custom-call(f32[1,1024]{1,0:T(1,128)} %bitcast.11, s32[1,64]{1,0:T(1,128)} %lengths_ref.1, s32[8,16]{1,0:T(8,128)} %wanted_ref.1, bf16[256,1024]{1,0:T(8,128)(2,1)} %bitcast.6, bf16[256,1024]{1,0:T(8,128)(2,1)} %bitcast.7, bf16[256,1024]{1,0:T(8,128)(2,1)} %bitcast.8, ...), custom_call_target="tpu_custom_call" | custom-call | tf_op jit(solution)/shard_map/block/pallas_call | solution.py:504
  60.0 1.4 %copy.13 = bf16[1,16,1024]{2,1,0:T(8,128)(2,1)} copy(bf16[1,16,1024]{2,1,0:T(8,128)(2,1)} %bitcast.10) | data formatting | bytes 65536
  61.3 1.2 %copy.14 = f32[1,16]{1,0:T(1,128)} copy(f32[1,16]{1,0:T(1,128)} %get-tuple-element.9) | data formatting | bytes 128

commit v4 on v3

--- a/solution.py
+++ b/solution.py
@@ -239,19 +239,48 @@
         def _():
             ask_one(g).start()
 
-    def attend_own(g):
+    lead = min(2, chunks)
+
+    def prepare(g):
         load(1, g).wait()
         load(2, g).wait()
         v_t[g] = v_own[g].T
-        mixed, stat = scores_to_partial(q_own[g], k_own.at[g], v_t.at[g], 0, head_size)
-        mix_own[g] = mixed
-        stat_own[g] = stat
-
-    def attend_first(g, carry):
+
+    def attend_own(g):
+        mix_own[g], stat_own[g] = scores_to_partial(
+            q_own[g], k_own.at[g], v_t.at[g], 0, head_size
+        )
+
+    def attend_one(g):
+        mix_one[g], stat_one[g] = scores_to_partial(
+            q_one[g], k_own.at[g], v_t.at[g], 1, head_size
+        )
+
+    def attend_two(g):
+        mixed, stat = scores_to_partial(q_two[g], k_own.at[g], v_t.at[g], 2, head_size)
+        two_out[g] = mixed.astype(BF16)
+        two_out_stat[g] = stat
+
+    for g in range(lead):
+        prepare(g)
+    for g in range(lead):
         attend_own(g)
+
+    def blank_one(g, carry):
+        q_one[g] = jnp.zeros((tok_rows, chunk_cols), BF16)
         return carry
 
-    lax.fori_loop(0, ahead, attend_first, 0)
+    def blank_two(g, carry):
+        q_two[g] = jnp.zeros((tok_rows, chunk_cols), BF16)
+        return carry
+
+    @pl.when(jnp.logical_not(has_right))
+    def _():
+        lax.fori_loop(0, chunks, blank_one, 0)
+
+    @pl.when(jnp.logical_not(has_right_two))
+    def _():
+        lax.fori_loop(0, chunks, blank_two, 0)
 
     def step(t, carry):
         fresh = t < chunks
@@ -272,15 +301,9 @@
             def _():
                 ask_one(t + ahead).start()
 
-        @pl.when((t >= 2) & (t < chunks + 2) & has_right_two)
-        def _():
-            g = t - 2
-            ask_two(g).wait_recv()
-            mixed, stat = scores_to_partial(q_two[g], k_own.at[g], v_t.at[g], 2, head_size)
-            two_out[g] = mixed.astype(BF16)
-            two_out_stat[g] = stat
-            for copy in give_two(g):
-                copy.start()
+        @pl.when(t + lead < chunks)
+        def _():
+            prepare(t + lead)
 
         @pl.when((t >= 4) & (t < chunks + 4) & has_right)
         def _():
@@ -306,15 +329,31 @@
             for copy in give_one(g):
                 copy.start()
 
-        @pl.when(fresh & has_right)
-        def _():
-            mixed, stat = scores_to_partial(q_one[t], k_own.at[t], v_t.at[t], 1, head_size)
-            mix_one[t] = mixed
-            stat_one[t] = stat
-
-        @pl.when(t + ahead < chunks)
-        def _():
-            attend_own(t + ahead)
+        @pl.when(t < 2)
+        def _():
+            attend_one(t)
+            attend_own(jnp.minimum(t + lead, chunks - 1))
+
+        twice = (t >= 2) & (t < chunks + 2) & has_right_two
+
+        @pl.when(twice)
+        def _():
+            ask_two(t - 2).wait_recv()
+
+        @pl.when((t >= 2) & fresh)
+        def _():
+            attend_one(t)
+            attend_two(t - 2)
+            attend_own(jnp.minimum(t + lead, chunks - 1))
+
+        @pl.when((t >= chunks) & (t < chunks + 2))
+        def _():
+            attend_two(t - 2)
+
+        @pl.when(twice)
+        def _():
+            for copy in give_two(t - 2):
+                copy.start()
 
         @pl.when((t >= 6) & (t < chunks + 6))
         def _():
@@ -403,6 +442,29 @@
         )
         copy.start()
         copies.append(copy)
+
+    def drain(g, carry):
+        @pl.when(has_left)
+        def _():
+            ask_one(g).wait_send()
+
+            @pl.when(has_right)
+            def _():
+                ask_two(g).wait_send()
+
+        @pl.when(has_right_two)
+        def _():
+            for copy in give_two(g):
+                copy.wait_send()
+
+        @pl.when(has_right)
+        def _():
+            for copy in give_one(g):
+                copy.wait_send()
+
+        return carry
+
+    lax.fori_loop(0, chunks, drain, 0)
     queue_load.wait()
     for copy in copies:
         copy.wait()
@@ -458,29 +520,6 @@
     losses_ref[...] = jnp.sum(
         jnp.where(diagonal, jnp.broadcast_to(loss_col, square), 0.0), axis=0, keepdims=True
     )
-
-    def drain(g, carry):
-        @pl.when(has_left)
-        def _():
-            ask_one(g).wait_send()
-
-            @pl.when(has_right)
-            def _():
-                ask_two(g).wait_send()
-
-        @pl.when(has_right_two)
-        def _():
-            for copy in give_two(g):
-                copy.wait_send()
-
-        @pl.when(has_right)
-        def _():
-            for copy in give_one(g):
-                copy.wait_send()
-
-        return carry
-
-    lax.fori_loop(0, chunks, drain, 0)
 
 
 def body(

time: 62.8 us -> 63.8 us (1.016)
  Pallas kernels: 59.3 us -> 60.4 us
    pallas_call x1, Pallas kernels: 59.3 us -> 60.4 us  [body(): pl.pallas_call(functools.partial(block_kernel, n_seq, n_batch, head_size)...]
where the time goes in v4:
time: 63.8 us; the launch traced here: 63.5 us
  Pallas kernels  60.4 us (95%)
  local copies, waits for them, and re-layouts  2.55 us (4%)
  between operations  0.64 us (1%)
    pallas_call x1, Pallas kernels, body(): pl.pallas_call(functools.partial(block_kernel, n_seq, n_batch, head_size)...  60.4 us
    unnamed x2, local copies, waits for them, and re-layouts  2.55 us

profile of v4, /device:TPU:0, one launch (start us, length us, event | category | flops | bytes accessed | tf_op | source)
XLA Modules:
  0.0 63.5 jit_solution(216102174574163852)
XLA Ops:
  0.6 60.4 %block.1 = (bf16[16,1024]{1,0:T(8,128)(2,1)}, f32[1,16]{1,0:T(1,128)}) custom-call(f32[1,1024]{1,0:T(1,128)} %bitcast.11, s32[1,64]{1,0:T(1,128)} %lengths_ref.1, s32[8,16]{1,0:T(8,128)} %wanted_ref.1, bf16[256,1024]{1,0:T(8,128)(2,1)} %bitcast.6, bf16[256,1024]{1,0:T(8,128)(2,1)} %bitcast.7, bf16[256,1024]{1,0:T(8,128)(2,1)} %bitcast.8, ...), custom_call_target="tpu_custom_call" | custom-call | tf_op jit(solution)/shard_map/block/pallas_call | solution.py:543
  61.0 1.4 %copy.13 = bf16[1,16,1024]{2,1,0:T(8,128)(2,1)} copy(bf16[1,16,1024]{2,1,0:T(8,128)(2,1)} %bitcast.10) | data formatting | bytes 65536
  62.4 1.2 %copy.14 = f32[1,16]{1,0:T(1,128)} copy(f32[1,16]{1,0:T(1,128)} %get-tuple-element.9) | data formatting | bytes 128
